TPU v7x, 32 devices: a whole 2x2x4 slice. The times are simulated.
32 devices in a mesh: dp: 8 (over z, x), mp: 4 (over y, core).
Axes of the slice: x: 2, y: 2, z: 4, core: 2. Of those that a mesh axis runs over, the one named last changes fastest.
Arguments:
- vision: bfloat16 [2048, 3200], P(('dp', 'mp')), may hold values from -6 to 6
- vision_gain: float32 [3200], replicated, may hold values from 0.1 to 1.9
- image_slot: int32 [8], replicated, may hold values from 0 to 15, as said below
- text_embed: bfloat16 [4096, 8192], P('dp', 'mp'), may hold values from -6 to 6
- w_proj: bfloat16 [3200, 8192], P(None, 'mp'), may hold values from -0.109375 to 0.109375
- llm_gain: float32 [8192], P('mp'), may hold values from 0.1 to 1.9
- w_key: bfloat16 [8192, 1024], P('mp'), may hold values from -0.0625 to 0.0625
- w_value: bfloat16 [8192, 1024], P('mp'), may hold values from -0.0625 to 0.0625
- key_grad: bfloat16 [4096, 1024], P('dp', 'mp'), may hold values from -6 to 6
- value_grad: bfloat16 [4096, 1024], P('dp', 'mp'), may hold values from -6 to 6
Outputs:
- key_out: bfloat16 [4096, 1024], P('dp', 'mp')
- value_out: bfloat16 [4096, 1024], P('dp', 'mp')
- text_grad: bfloat16 [4096, 8192], P('dp', 'mp')
- vision_grad: bfloat16 [2048, 3200], P(('dp', 'mp'))
Inputs may be any that keep to these rules, and one draw needn't show every extreme that they name: `image_slot`: the 8 entries are different slots. Image i is encoded on index i of dp; slot j covers positions j * 256 to (j + 1) * 256 - 1, so it lies on index j // 2 of dp. One index of dp receives 2 images, every other one at most one.
All inputs are finite; a program needn't handle non-finite values.
Results may differ from a plain program's by a relative error of at most 0.0058.
Values may be sent and summed in bfloat16 or wider, within the bound.
A program may use at most 128 MiB of HBM per device.

v0:
```python
import functools

import jax
import jax.numpy as jnp
from jax import lax
from jax.experimental import pallas as pl
from jax.experimental.pallas import tpu as pltpu
from jax.sharding import PartitionSpec as P

PATCH = 256
F32 = jnp.float32
BF16 = jnp.bfloat16
NT = (((1,), (1,)), ((), ()))
DMA = pltpu.SemaphoreType.DMA


def nt(a, b):
    return lax.dot_general(a, b, NT, preferred_element_type=F32)


def remote(src, dst, send_sem, recv_sem, device):
    return pltpu.make_async_remote_copy(
        src_ref=src, dst_ref=dst, send_sem=send_sem, recv_sem=recv_sem,
        device_id=device, device_id_type=pl.DeviceIdType.MESH,
    )


def to_rows(sq, inner):
    lane = lax.broadcasted_iota(jnp.int32, (sq.shape[0], 128), 1)
    wide = jnp.where(lane == 0, sq, jnp.where(lane == 1, inner, 0.0))
    return jnp.transpose(wide)[:8]


def to_columns(rows):
    wide = jnp.transpose(jnp.concatenate([rows] * 16, axis=0))
    return wide[:, 0:1], wide[:, 1:2]


def kernel(
    dp, mp, slot_ref, vision_h, vgain, text_h, wp_h, gain, wk_h, wv_h, kg_h, vg_h, kg4, vg4,
    k_out, v_out, tg_h, vg_out,
    vis, vis_all, text, wp, wk, wv, xt, gk, gv, gik, giv, emb, xi, dimg, dg,
    t_send, t_own, t_l1, t_s2, t_l2, i_send, i_own, i_l1, i_s2, i_l2,
    d_send, d_own, d_l1, d_s2, d_l2, kvt, kvi,
    st_t, sr_t, st_i, sr_i, sc_t, co_t, sc_i, co_i,
    r1k, r1v, s2k, s2v, r2k, r2v, kvb, r3, s4, r4, tg,
    load_sem, ag_s, ag_r, rs_s, rs_r, st_s, st_r, dv_s, dv_r,
    a1_s, a1_r, a2_s, a2_r, b1_s, b1_r, b2_s, b2_r, tg_sem, dt,
):
    me_d = lax.axis_index("dp")
    me = lax.axis_index("mp")
    ycount = mp // 2
    core = lax.rem(me, 2)
    y = lax.div(me, 2)
    partner = y * 2 + (1 - core)
    tokens, width = text.shape
    slots = tokens // PATCH
    kvd = gk.shape[1] // mp
    rows = vis.shape[0]
    dv = vis.shape[1]
    d_model = width * mp
    rb = r1k.shape[1]

    def ynext(k):
        return lax.rem(y + k, ycount)

    def yprev(k):
        return lax.rem(y + ycount - k, ycount)

    def dnext(k):
        return lax.rem(me_d + k, dp)

    def dprev(k):
        return lax.rem(me_d + dp - k, dp)

    def col(m):
        return pl.ds(pl.multiple_of(m * kvd, kvd), kvd)

    def owner_of(slot):
        found = jnp.int32(0)
        for i in range(dp):
            found = jnp.where(slot_ref[i] == slot, jnp.int32(i), found)
        return found

    def filled(s):
        found = jnp.int32(0)
        for i in range(dp):
            found = jnp.where(slot_ref[i] == me_d * slots + s, jnp.int32(1), found)
        return found.astype(F32)

    sends = []

    def send(*args):
        copy = remote(*args)
        copy.start()
        sends.append(copy)

    loads = [
        (vision_h, vis), (kg_h, gk.at[:, col(me)]), (vg_h, gv.at[:, col(me)]),
        (text_h, text), (wk_h, wk), (wv_h, wv), (wp_h, wp),
        (kg4.at[:, me_d], r1k.at[pl.ds(me_d * slots, slots)]),
        (vg4.at[:, me_d], r1v.at[pl.ds(me_d * slots, slots)]),
    ]
    loads = [pltpu.make_async_copy(a, b, load_sem.at[n]) for n, (a, b) in enumerate(loads)]
    for copy in loads:
        copy.start()

    barrier = pltpu.get_barrier_semaphore()

    @pl.loop(1, dp)
    def _(k):
        pl.semaphore_signal(barrier, inc=1, device_id=(dnext(k), me), device_id_type=pl.DeviceIdType.MESH)

    for k in range(1, mp):
        pl.semaphore_signal(
            barrier, inc=1, device_id=(me_d, lax.rem(me + k, mp)), device_id_type=pl.DeviceIdType.MESH
        )

    loads[0].wait()
    vf = vis[...].astype(F32)
    vscale = lax.rsqrt(jnp.mean(vf * vf, axis=1, keepdims=True) + 1e-06)
    vis_all[me] = (vf * vscale * vgain[...]).astype(BF16)
    pl.semaphore_wait(barrier, dp - 1 + mp - 1)

    def gather_start(g, block):
        for k in range(1, ycount):
            send(block(me), block(me), ag_s.at[g, 0, k], ag_r.at[g, 0, k], (me_d, ynext(k) * 2 + core))
        send(block(me), block(me), ag_s.at[g, 0, 0], ag_r.at[g, 0, 0], (me_d, partner))

    def arrived(block, send_sem, recv_sem):
        remote(block, block, send_sem, recv_sem, (me_d, partner)).wait_recv()

    def gather_relay(g, block):
        for k in range(1, ycount):
            got = block(yprev(k) * 2 + core)
            arrived(got, ag_s.at[g, 0, k], ag_r.at[g, 0, k])
            send(got, got, ag_s.at[g, 1, k], ag_r.at[g, 1, k], (me_d, partner))

    def gather_finish(g, block):
        arrived(block(partner), ag_s.at[g, 0, 0], ag_r.at[g, 0, 0])
        for k in range(1, ycount):
            arrived(block(yprev(k) * 2 + 1 - core), ag_s.at[g, 1, k], ag_r.at[g, 1, k])

    vis_block = lambda m: vis_all.at[m]
    gk_block = lambda m: gk.at[:, col(m)]
    gv_block = lambda m: gv.at[:, col(m)]
    gik_block = lambda m: gik.at[:, col(m)]
    giv_block = lambda m: giv.at[:, col(m)]

    gather_start(0, vis_block)

    mine = pl.ds(me_d * slots, slots)

    def a1(k, which):
        src, dst = ((kg4, r1k), (vg4, r1v))[which]
        return remote(
            src.at[:, dnext(k)], dst.at[mine], a1_s.at[which, k], a1_r.at[which, k], (dnext(k), me)
        )

    @pl.loop(1, dp)
    def _(k):
        a1(k, 0).start()
        a1(k, 1).start()

    loads[1].wait()
    loads[2].wait()
    gather_start(1, gk_block)
    gather_start(2, gv_block)

    def stage(x, n, psend, own, l1):
        def chunk(m):
            k_part = jnp.dot(x[...], wk[:, col(m)], preferred_element_type=F32)
            v_part = jnp.dot(x[...], wv[:, col(m)], preferred_element_type=F32)
            return k_part, v_part

        for k in range(ycount):
            yk = ynext(k)
            k_part, v_part = chunk(yk * 2 + 1 - core)
            psend[yk, :, :kvd] = k_part.astype(BF16)
            psend[yk, :, kvd:] = v_part.astype(BF16)
            send(psend.at[yk], l1.at[yk], rs_s.at[n, 0, k], rs_r.at[n, 0, k], (me_d, partner))
        for k in range(ycount):
            yk = ynext(k)
            k_part, v_part = chunk(yk * 2 + core)
            own[yk, :, :kvd] = k_part
            own[yk, :, kvd:] = v_part

    def level_two(n, own, l1, s2, l2):
        for k in range(ycount - 1, 0, -1):
            yk = ynext(k)
            arrived(l1.at[yk], rs_s.at[n, 0, k], rs_r.at[n, 0, k])
            s2[k] = (own[yk] + l1[yk].astype(F32)).astype(BF16)

    def level_go(n, s2, l2):
        for k in range(ycount - 1, 0, -1):
            send(s2.at[k], l2.at[k], rs_s.at[n, 1, k], rs_r.at[n, 1, k], (me_d, ynext(k) * 2 + core))

    def level_end(n, own, l1, l2):
        arrived(l1.at[y], rs_s.at[n, 0, 0], rs_r.at[n, 0, 0])
        total = own[y] + l1[y].astype(F32)
        for k in range(1, ycount):
            arrived(l2.at[k], rs_s.at[n, 1, k], rs_r.at[n, 1, k])
            total = total + l2[k].astype(F32)
        return total

    def stats_send(n, st, sr):
        for k in range(1, mp):
            send(st, sr.at[k], st_s.at[n, k], st_r.at[n, k], (me_d, lax.rem(me + k, mp)))

    def stats_end(n, st, sr, sc, co, keep):
        total = st[...]
        for k in range(1, mp):
            arrived(sr.at[k], st_s.at[n, k], st_r.at[n, k])
            total = total + sr[k]
        sq, inner = to_columns(total)
        scale = lax.rsqrt(sq / d_model + 1e-05)
        sc[...] = jnp.broadcast_to(scale * keep, sc.shape)
        co[...] = jnp.broadcast_to(scale * scale * scale * (inner / d_model) * keep, co.shape)

    loads[3].wait()
    tf = text[...].astype(F32)
    sq_t = jnp.sum(tf * tf, axis=1, keepdims=True)
    xt[...] = (tf * gain[...]).astype(BF16)
    loads[4].wait()
    loads[5].wait()
    stage(xt, 0, t_send, t_own, t_l1)
    gather_relay(0, vis_block)
    level_two(0, t_own, t_l1, t_s2, t_l2)

    gather_finish(0, vis_block)
    loads[6].wait()
    step = 256
    dimg_rows = mp * rows


    def project(j, acc):
        cs = pl.ds(pl.multiple_of(j * step, step), step)
        e = jnp.concatenate([vis_all[m] for m in range(mp)], axis=0)
        e = jnp.dot(e, wp[:, cs], preferred_element_type=F32).astype(BF16)
        emb[:, cs] = e
        ef = e.astype(F32)
        xi[:, cs] = (ef * gain[:, cs]).astype(BF16)
        return acc + jnp.sum(ef * ef, axis=1, keepdims=True)

    half = width // step // 2
    sq_i = lax.fori_loop(0, half, project, jnp.zeros((dimg_rows, 1), F32))

    loads[7].wait()
    loads[8].wait()

    @pl.loop(1, dp)
    def _(k):
        for which, dst in ((0, r1k), (1, r1v)):
            block = dst.at[pl.ds(dprev(k) * slots, slots)]
            remote(block, block, a1_s.at[which, k], a1_r.at[which, k], (me_d, partner)).wait_recv()

    @pl.loop(0, dp)
    def _(i):
        s2k[i] = r1k[slot_ref[i]]
        s2v[i] = r1v[slot_ref[i]]

    r2k[me_d] = s2k[me_d]
    r2v[me_d] = s2v[me_d]

    def a2(k, which):
        src, dst = ((s2k, r2k), (s2v, r2v))[which]
        return remote(
            src.at[dnext(k)], dst.at[me_d], a2_s.at[which, k], a2_r.at[which, k], (dnext(k), me)
        )

    @pl.loop(1, dp)
    def _(k):
        a2(k, 0).start()
        a2(k, 1).start()

    sq_i = lax.fori_loop(half, width // step, project, sq_i)
    stage(xi, 1, i_send, i_own, i_l1)
    level_two(1, i_own, i_l1, i_s2, i_l2)
    level_go(1, i_s2, i_l2)

    @pl.loop(1, dp)
    def _(k):
        for which, dst in ((0, r2k), (1, r2v)):
            block = dst.at[dprev(k)]
            remote(block, block, a2_s.at[which, k], a2_r.at[which, k], (me_d, partner)).wait_recv()

    own_k = r2k[...].astype(F32).reshape(PATCH, kvd)
    own_v = r2v[...].astype(F32).reshape(PATCH, kvd)
    gik[:, col(me)] = own_k.astype(BF16)
    giv[:, col(me)] = own_v.astype(BF16)
    gather_start(3, gik_block)
    gather_start(4, giv_block)
    level_go(0, t_s2, t_l2)
    gather_relay(1, gk_block)
    gather_relay(2, gv_block)
    gather_finish(1, gk_block)
    gather_finish(2, gv_block)

    def text_product(j, _):
        cs = pl.ds(pl.multiple_of(j * step, step), step)
        dt[:, cs] = (nt(gk[...], wk[cs, :]) + nt(gv[...], wv[cs, :])) * gain[:, cs]
        return 0

    lax.fori_loop(0, width // step, text_product, 0)

    total = level_end(1, i_own, i_l1, i_l2)
    kvi[...] = total
    inner = jnp.sum(
        total[:, :kvd] * gik[:, col(me)].astype(F32) + total[:, kvd:] * giv[:, col(me)].astype(F32),
        axis=1, keepdims=True,
    )
    st_i[...] = to_rows(sq_i, inner)
    stats_send(1, st_i, sr_i)
    gather_relay(3, gik_block)
    gather_relay(4, giv_block)
    gather_finish(3, gik_block)
    gather_finish(4, giv_block)

    def image_back(j, _):
        cs = pl.ds(pl.multiple_of(j * step, step), step)
        dg[:, cs] = (nt(gik[...], wk[cs, :]) + nt(giv[...], wv[cs, :])) * gain[:, cs]
        return 0

    lax.fori_loop(0, width // step, image_back, 0)
    stats_end(1, st_i, sr_i, sc_i, co_i, 1.0)
    kvb[...] = (kvi[...] * sc_i[:, 0:1]).reshape(dp, rb, 2 * kvd).astype(BF16)
    r3[me_d] = kvb[me_d]

    def b1(k):
        return remote(kvb.at[dnext(k)], r3.at[me_d], b1_s.at[k], b1_r.at[k], (dnext(k), me))

    @pl.loop(1, dp)
    def _(k):
        b1(k).start()

    def image_end(j, _):
        cs = pl.ds(pl.multiple_of(j * step, step), step)
        d = sc_i[:, 0:1] * dg[:, cs] - emb[:, cs].astype(F32) * co_i[:, 0:1]
        dimg[:, cs] = d.astype(BF16)
        return 0

    lax.fori_loop(0, width // step, image_end, 0)

    pieces = d_send.shape[0]
    span = dv // pieces

    def vis_chunk(j):
        d = nt(dimg[...], wp[j * span:(j + 1) * span, :]).reshape(ycount, 2, rows, span)
        for yi in range(ycount):
            a, b = d[yi, 0], d[yi, 1]
            first = core == 0
            d_own[j, yi] = jnp.where(first, a, b)
            d_send[j, yi] = jnp.where(first, b, a).astype(BF16)
        send(d_send.at[j], d_l1.at[j], dv_s.at[0, j, 0], dv_r.at[0, j, 0], (me_d, partner))

    def vis_two(j):
        arrived(d_l1.at[j], dv_s.at[0, j, 0], dv_r.at[0, j, 0])
        for k in range(1, ycount):
            yk = ynext(k)
            d_s2[j, k] = (d_own[j, yk] + d_l1[j, yk].astype(F32)).astype(BF16)
            send(d_s2.at[j, k], d_l2.at[j, k], dv_s.at[1, j, k], dv_r.at[1, j, k], (me_d, yk * 2 + core))

    def b2(k):
        return remote(s4.at[dnext(k)], r4.at[:, me_d], b2_s.at[k], b2_r.at[k], (dnext(k), me))

    for j in range(pieces):
        vis_chunk(j)
        if j > 0:
            vis_two(j - 1)
        if j == min(2, pieces - 1):

            @pl.loop(1, dp)
            def _(k):
                block = r3.at[dprev(k)]
                remote(block, block, b1_s.at[k], b1_r.at[k], (me_d, partner)).wait_recv()

            @pl.loop(0, dp)
            def _(d):
                for s in range(slots):
                    s4[d, s] = r3[owner_of(d * slots + s)]

            for s in range(slots):
                r4[s, me_d] = s4[me_d, s]

            @pl.loop(1, dp)
            def _(k):
                b2(k).start()

    vis_two(pieces - 1)

    total = level_end(0, t_own, t_l1, t_l2)
    kvt[...] = total
    inner = jnp.sum(
        total[:, :kvd] * gk[:, col(me)].astype(F32) + total[:, kvd:] * gv[:, col(me)].astype(F32),
        axis=1, keepdims=True,
    )
    st_t[...] = to_rows(sq_t, inner)
    stats_send(0, st_t, sr_t)
    keep = jnp.concatenate([jnp.full((PATCH, 1), 1.0, F32) * (1.0 - filled(s)) for s in range(slots)], axis=0)
    stats_end(0, st_t, sr_t, sc_t, co_t, keep)

    def text_copy(j):
        cs = pl.ds(pl.multiple_of(j * step, step), step)
        return pltpu.make_async_copy(tg.at[:, cs], tg_h.at[:, cs], tg_sem.at[j])

    def text_back(j, _):
        cs = pl.ds(pl.multiple_of(j * step, step), step)
        d = sc_t[:, 0:1] * dt[:, cs] - text[:, cs].astype(F32) * co_t[:, 0:1]
        tg[:, cs] = d.astype(BF16)
        text_copy(j).start()
        return 0

    lax.fori_loop(0, width // step, text_back, 0)

    hs = []
    for j in range(pieces):
        d = d_own[j, y] + d_l1[j, y].astype(F32)
        for k in range(1, ycount):
            arrived(d_l2.at[j, k], dv_s.at[1, j, k], dv_r.at[1, j, k])
            d = d + d_l2[j, k].astype(F32)
        hs.append(d.astype(BF16).astype(F32))
    vf = vis[...].astype(F32)
    vscale = lax.rsqrt(jnp.mean(vf * vf, axis=1, keepdims=True) + 1e-06)
    h = jnp.concatenate(hs, axis=1) * vgain[...]
    v_inner = jnp.mean(h * vf, axis=1, keepdims=True)
    vg_out[...] = (vscale * h - vf * vscale * vscale * vscale * v_inner).astype(BF16)

    @pl.loop(1, dp)
    def _(k):
        block = r4.at[:, dprev(k)]
        remote(block, block, b2_s.at[k], b2_r.at[k], (me_d, partner)).wait_recv()

    for s in range(slots):
        at = pl.ds(s * PATCH, PATCH)
        out = kvt[at, :] * sc_t[at, 0:1] + r4[s].astype(F32).reshape(PATCH, 2 * kvd) * filled(s)
        k_out[at, :] = out[:, :kvd].astype(BF16)
        v_out[at, :] = out[:, kvd:].astype(BF16)

    for copy in sends:
        copy.wait_send()

    @pl.loop(1, dp)
    def _(k):
        a1(k, 0).wait_send()
        a1(k, 1).wait_send()
        a2(k, 0).wait_send()
        a2(k, 1).wait_send()
        b1(k).wait_send()
        b2(k).wait_send()

    @pl.loop(0, width // step)
    def _(j):
        text_copy(j).wait()


def shards(vision, vision_gain, image_slot, text_embed, w_proj, llm_gain, w_key, w_value, key_grad, value_grad):
    dp = lax.axis_size("dp")
    mp = lax.axis_size("mp")
    tokens, width = text_embed.shape
    slots = tokens // PATCH
    rows, dv = vision.shape
    kvd = key_grad.shape[1]
    kv = kvd * mp
    img = rows * mp
    rb = PATCH // dp
    ys = mp // 2
    pieces = 5 if dv % 640 == 0 else 1
    span = dv // pieces
    V = pltpu.VMEM
    any_spec = pl.BlockSpec(memory_space=pl.ANY)
    vmem = pl.BlockSpec(memory_space=pltpu.VMEM)
    smem = pl.BlockSpec(memory_space=pltpu.SMEM)
    scratch = [
        V((rows, dv), BF16), V((mp, rows, dv), BF16), V((tokens, width), BF16), V((dv, width), BF16),
        V((width, kv), BF16), V((width, kv), BF16), V((tokens, width), BF16),
        V((tokens, kv), BF16), V((tokens, kv), BF16), V((img, kv), BF16), V((img, kv), BF16),
        V((img, width), BF16), V((img, width), BF16), V((img, width), BF16), V((img, width), F32),
    ]
    for n in (tokens, img):
        scratch += [
            V((ys, n, 2 * kvd), BF16), V((ys, n, 2 * kvd), F32), V((ys, n, 2 * kvd), BF16),
            V((ys, n, 2 * kvd), BF16), V((ys, n, 2 * kvd), BF16),
        ]
    scratch += [
        V((pieces, ys, rows, span), BF16), V((pieces, ys, rows, span), F32), V((pieces, ys, rows, span), BF16),
        V((pieces, ys, rows, span), BF16), V((pieces, ys, rows, span), BF16),
        V((tokens, 2 * kvd), F32), V((img, 2 * kvd), F32),
        V((8, tokens), F32), V((mp, 8, tokens), F32), V((8, img), F32), V((mp, 8, img), F32),
        V((tokens, 128), F32), V((tokens, 128), F32), V((img, 128), F32), V((img, 128), F32),
        V((dp * slots, rb, kvd), BF16), V((dp * slots, rb, kvd), BF16),
        V((dp, rb, kvd), BF16), V((dp, rb, kvd), BF16), V((dp, rb, kvd), BF16), V((dp, rb, kvd), BF16),
        V((dp, rb, 2 * kvd), BF16), V((dp, rb, 2 * kvd), BF16),
        V((dp, slots, rb, 2 * kvd), BF16), V((slots, dp, rb, 2 * kvd), BF16),
        V((tokens, width), BF16),
        DMA((9,)), DMA((5, 2, ys)), DMA((5, 2, ys)), DMA((2, 2, ys)), DMA((2, 2, ys)),
        DMA((2, mp)), DMA((2, mp)), DMA((2, pieces, ys)), DMA((2, pieces, ys)),
        DMA((2, dp)), DMA((2, dp)), DMA((2, dp)), DMA((2, dp)),
        DMA((dp,)), DMA((dp,)), DMA((dp,)), DMA((dp,)), DMA((width // 256,)), V((tokens, width), F32),
    ]
    return pl.pallas_call(
        functools.partial(kernel, dp, mp),
        out_shape=(
            jax.ShapeDtypeStruct((tokens, kvd), BF16),
            jax.ShapeDtypeStruct((tokens, kvd), BF16),
            jax.ShapeDtypeStruct((tokens, width), BF16),
            jax.ShapeDtypeStruct((rows, dv), BF16),
        ),
        in_specs=[smem, any_spec, vmem, any_spec, any_spec, vmem] + [any_spec] * 6,
        out_specs=(vmem, vmem, any_spec, vmem),
        scratch_shapes=scratch,
        compiler_params=pltpu.CompilerParams(
            collective_id=0, has_side_effects=True, vmem_limit_bytes=67043328
        ),
    )(
        image_slot, vision, vision_gain[None, :], text_embed, w_proj, llm_gain[None, :],
        w_key, w_value, key_grad, value_grad,
        key_grad.reshape(slots, dp, rb, kvd), value_grad.reshape(slots, dp, rb, kvd),
    )


def solution(mesh):
    placed = (
        P(("dp", "mp"), None),
        P(),
        P(),
        P("dp", "mp"),
        P(None, "mp"),
        P("mp"),
        P("mp", None),
        P("mp", None),
        P("dp", "mp"),
        P("dp", "mp"),
    )
    return jax.shard_map(
        shards,
        mesh=mesh,
        in_specs=placed,
        out_specs=(P("dp", "mp"), P("dp", "mp"), P("dp", "mp"), P(("dp", "mp"), None)),
        check_vma=False,
    )
```

profile of v0, /device:TPU:0, one launch (start us, length us, event | category | flops | bytes accessed | tf_op | source)
XLA Modules:
  0.0 84.5 jit_solution(161730307703553798)
XLA Ops:
  0.6 1.3 %broadcast_in_dim.6.vgain = f32[1,3200]{1,0:T(1,128)} reshape(f32[3200]{0:T(1024)} %param.11) | data formatting | bytes 25600 | tf_op jit(solution)/shard_map/broadcast_in_dim | solution.py:515
  2.0 75.2 %shard_map.129 = (bf16[512,256]{1,0:T(8,128)(2,1)}, bf16[512,256]{1,0:T(8,128)(2,1)}, bf16[512,2048]{1,0:T(8,128)(2,1)}, bf16[64,3200]{1,0:T(8,128)(2,1)}) custom-call(s32[8]{0:T(128)} %slot_ref.1, bf16[64,3200]{1,0:T(8,128)(2,1)} %vision_h.1, f32[1,3200]{1,0:T(1,128)} %broadcast_in_dim.6.vgain, bf16[512,2048]{1,0:T(8,128)(2,1)} %text_h.1, ...), custom_call_target="tpu_custom_call" | custom-call | tf_op jit(solution)/shard_map/pallas_call | solution.py:500
  77.1 0.0 copy-start
  77.2 1.7 %copy.18 = bf16[512,256]{1,0:T(8,128)(2,1)} copy(bf16[512,256]{1,0:T(8,128)(2,1)} %get-tuple-element.8) | data formatting | bytes 524288
  78.9 1.7 %copy.19 = bf16[512,256]{1,0:T(8,128)(2,1)} copy(bf16[512,256]{1,0:T(8,128)(2,1)} %get-tuple-element.9) | data formatting | bytes 524288
  80.5 3.2 %copy.20 = bf16[512,2048]{1,0:T(8,128)(2,1)} copy(bf16[512,2048]{1,0:T(8,128)(2,1)} %get-tuple-element.10) | data formatting | bytes 4194304
  83.7 0.0 copy-done
  83.7 0.8 copy.21
Async XLA Ops:
  77.1 6.6 %copy-start = (bf16[64,3200]{1,0:T(8,128)(2,1)S(1)}, bf16[64,3200]{1,0:T(8,128)(2,1)}, u32[]{:S(2)}) copy-start(bf16[64,3200]{1,0:T(8,128)(2,1)} %get-tuple-element.11) | copy-start | bytes 1228804
where the time goes:
time: 84.8 us; the launch traced here: 84.5 us
  Pallas kernels  75.2 us (89%)
  local copies, waits for them, and re-layouts  8.63 us (10%)
    pallas_call x1, Pallas kernels, shards(): pl.pallas_call(functools.partial(kernel, dp, mp), out_shape=(jax.ShapeDty...  75.2 us
    unnamed x6, local copies, waits for them, and re-layouts  7.3 us

commit v1 on v0

--- a/solution.py
+++ b/solution.py
@@ -36,16 +36,31 @@
     return wide[:, 0:1], wide[:, 1:2]
 
 
+def gain_row(ref):
+    if ref.shape[0] == 1:
+        return ref[...]
+    return jnp.concatenate([ref[i:i + 1, :] for i in range(ref.shape[0])], axis=1)
+
+
+def write_out(*refs):
+    count = (len(refs) - 1) // 2
+    copies = [pltpu.make_async_copy(refs[n], refs[count + n], refs[-1].at[n]) for n in range(count)]
+    for copy in copies:
+        copy.start()
+    for copy in copies:
+        copy.wait()
+
+
 def kernel(
     dp, mp, slot_ref, vision_h, vgain, text_h, wp_h, gain, wk_h, wv_h, kg_h, vg_h, kg4, vg4,
-    k_out, v_out, tg_h, vg_out,
+    k_out, v_out, tg, vg_out,
     vis, vis_all, text, wp, wk, wv, xt, gk, gv, gik, giv, emb, xi, dimg, dg,
     t_send, t_own, t_l1, t_s2, t_l2, i_send, i_own, i_l1, i_s2, i_l2,
     d_send, d_own, d_l1, d_s2, d_l2, kvt, kvi,
     st_t, sr_t, st_i, sr_i, sc_t, co_t, sc_i, co_i,
-    r1k, r1v, s2k, s2v, r2k, r2v, kvb, r3, s4, r4, tg,
+    r1k, r1v, s2k, s2v, r2k, r2v, kvb, r3, s4, r4,
     load_sem, ag_s, ag_r, rs_s, rs_r, st_s, st_r, dv_s, dv_r,
-    a1_s, a1_r, a2_s, a2_r, b1_s, b1_r, b2_s, b2_r, tg_sem, dt,
+    a1_s, a1_r, a2_s, a2_r, b1_s, b1_r, b2_s, b2_r, dt,
 ):
     me_d = lax.axis_index("dp")
     me = lax.axis_index("mp")
@@ -119,7 +134,8 @@
     loads[0].wait()
     vf = vis[...].astype(F32)
     vscale = lax.rsqrt(jnp.mean(vf * vf, axis=1, keepdims=True) + 1e-06)
-    vis_all[me] = (vf * vscale * vgain[...]).astype(BF16)
+    vis_gain = gain_row(vgain)
+    vis_all[me] = (vf * vscale * vis_gain).astype(BF16)
     pl.semaphore_wait(barrier, dp - 1 + mp - 1)
 
     def gather_start(g, block):
@@ -399,15 +415,10 @@
     keep = jnp.concatenate([jnp.full((PATCH, 1), 1.0, F32) * (1.0 - filled(s)) for s in range(slots)], axis=0)
     stats_end(0, st_t, sr_t, sc_t, co_t, keep)
 
-    def text_copy(j):
-        cs = pl.ds(pl.multiple_of(j * step, step), step)
-        return pltpu.make_async_copy(tg.at[:, cs], tg_h.at[:, cs], tg_sem.at[j])
-
     def text_back(j, _):
         cs = pl.ds(pl.multiple_of(j * step, step), step)
         d = sc_t[:, 0:1] * dt[:, cs] - text[:, cs].astype(F32) * co_t[:, 0:1]
         tg[:, cs] = d.astype(BF16)
-        text_copy(j).start()
         return 0
 
     lax.fori_loop(0, width // step, text_back, 0)
@@ -421,7 +432,7 @@
         hs.append(d.astype(BF16).astype(F32))
     vf = vis[...].astype(F32)
     vscale = lax.rsqrt(jnp.mean(vf * vf, axis=1, keepdims=True) + 1e-06)
-    h = jnp.concatenate(hs, axis=1) * vgain[...]
+    h = jnp.concatenate(hs, axis=1) * gain_row(vgain)
     v_inner = jnp.mean(h * vf, axis=1, keepdims=True)
     vg_out[...] = (vscale * h - vf * vscale * vscale * vscale * v_inner).astype(BF16)
 
@@ -447,10 +458,6 @@
         a2(k, 1).wait_send()
         b1(k).wait_send()
         b2(k).wait_send()
-
-    @pl.loop(0, width // step)
-    def _(j):
-        text_copy(j).wait()
 
 
 def shards(vision, vision_gain, image_slot, text_embed, w_proj, llm_gain, w_key, w_value, key_grad, value_grad):
@@ -491,31 +498,36 @@
         V((dp, rb, kvd), BF16), V((dp, rb, kvd), BF16), V((dp, rb, kvd), BF16), V((dp, rb, kvd), BF16),
         V((dp, rb, 2 * kvd), BF16), V((dp, rb, 2 * kvd), BF16),
         V((dp, slots, rb, 2 * kvd), BF16), V((slots, dp, rb, 2 * kvd), BF16),
-        V((tokens, width), BF16),
         DMA((9,)), DMA((5, 2, ys)), DMA((5, 2, ys)), DMA((2, 2, ys)), DMA((2, 2, ys)),
         DMA((2, mp)), DMA((2, mp)), DMA((2, pieces, ys)), DMA((2, pieces, ys)),
         DMA((2, dp)), DMA((2, dp)), DMA((2, dp)), DMA((2, dp)),
-        DMA((dp,)), DMA((dp,)), DMA((dp,)), DMA((dp,)), DMA((width // 256,)), V((tokens, width), F32),
+        DMA((dp,)), DMA((dp,)), DMA((dp,)), DMA((dp,)), V((tokens, width), F32),
     ]
-    return pl.pallas_call(
+    shapes = ((tokens, kvd), (tokens, kvd), (tokens, width), (rows, dv))
+    room = sum(2 * a * b for a, b in shapes)
+    lanes = 128 if dv % 128 == 0 else dv
+    results = pl.pallas_call(
         functools.partial(kernel, dp, mp),
-        out_shape=(
-            jax.ShapeDtypeStruct((tokens, kvd), BF16),
-            jax.ShapeDtypeStruct((tokens, kvd), BF16),
-            jax.ShapeDtypeStruct((tokens, width), BF16),
-            jax.ShapeDtypeStruct((rows, dv), BF16),
-        ),
+        out_shape=tuple(V(shape, BF16) for shape in shapes),
         in_specs=[smem, any_spec, vmem, any_spec, any_spec, vmem] + [any_spec] * 6,
-        out_specs=(vmem, vmem, any_spec, vmem),
+        out_specs=(vmem,) * len(shapes),
         scratch_shapes=scratch,
         compiler_params=pltpu.CompilerParams(
-            collective_id=0, has_side_effects=True, vmem_limit_bytes=67043328
+            collective_id=0, has_side_effects=True, vmem_limit_bytes=67043328 - room
         ),
     )(
-        image_slot, vision, vision_gain[None, :], text_embed, w_proj, llm_gain[None, :],
+        image_slot, vision, vision_gain.reshape(-1, lanes), text_embed, w_proj, llm_gain[None, :],
         w_key, w_value, key_grad, value_grad,
         key_grad.reshape(slots, dp, rb, kvd), value_grad.reshape(slots, dp, rb, kvd),
     )
+    return pl.pallas_call(
+        write_out,
+        out_shape=tuple(jax.ShapeDtypeStruct(shape, BF16) for shape in shapes),
+        in_specs=[vmem] * len(shapes),
+        out_specs=(any_spec,) * len(shapes),
+        scratch_shapes=[DMA((len(shapes),))],
+        compiler_params=pltpu.CompilerParams(vmem_limit_bytes=1 << 20),
+    )(*results)
 
 
 def solution(mesh):

time: 84.8 us -> 76.7 us (0.904)
  local copies, waits for them, and re-layouts: 8.63 us -> 0 us
    unnamed x6 -> x0, local copies, waits for them, and re-layouts: 7.3 us -> none
    broadcast_in_dim x1 -> x0, local copies, waits for them, and re-layouts: 1.33 us -> none  [shards(): vision_gain[None, :]]
    pallas_call x1 -> x2, Pallas kernels: 75.2 us -> 75.7 us  [the longest x1 74.1 us: shards(): pl.pallas_call(functools.partial(kernel, dp, mp), out_shape=tuple((V(shap...]
where the time goes in v1:
time: 76.7 us; the launch traced here: 76.5 us
  Pallas kernels  75.7 us (99%)
  between operations  0.8 us (1%)
    pallas_call x1, Pallas kernels, shards(): pl.pallas_call(functools.partial(kernel, dp, mp), out_shape=tuple((V(shap...  74.1 us
    pallas_call x1, Pallas kernels, shards(): pl.pallas_call(write_out, out_shape=tuple((jax.ShapeDtypeStruct(shape, BF...  1.65 us

profile of v1, /device:TPU:0, one launch (start us, length us, event | category | flops | bytes accessed | tf_op | source)
XLA Modules:
  0.0 76.5 jit_solution(3743314189713604480)
XLA Ops:
  0.6 74.1 %shard_map.129 = (bf16[512,256]{1,0:T(8,128)(2,1)S(1)}, bf16[512,256]{1,0:T(8,128)(2,1)S(1)}, bf16[512,2048]{1,0:T(8,128)(2,1)S(1)}, bf16[64,3200]{1,0:T(8,128)(2,1)S(1)}) custom-call(s32[8]{0:T(128)} %slot_ref.1, bf16[64,3200]{1,0:T(8,128)(2,1)} %vision_h.1, f32[25,128]{1,0:T(8,128)} %bitcast.6, bf16[512,2048]{1,0:T(8,128)(2,1)} %text_h.1, ...), custom_call_target="tpu_custom_call" | custom-call | tf_op jit(solution)/shard_map/pallas_call | solution.py:509
  74.7 1.7 %shard_map.130 = (bf16[512,256]{1,0:T(8,128)(2,1)}, bf16[512,256]{1,0:T(8,128)(2,1)}, bf16[512,2048]{1,0:T(8,128)(2,1)}, bf16[64,3200]{1,0:T(8,128)(2,1)}) custom-call(bf16[512,256]{1,0:T(8,128)(2,1)S(1)} %get-tuple-element.8.refs_0_, bf16[512,256]{1,0:T(8,128)(2,1)S(1)} %get-tuple-element.9.refs_1_, bf16[512,2048]{1,0:T(8,128)(2,1)S(1)} %get-tuple-element.10.refs_2_, ...), custom_call_target="tpu_custom_call" | custom-call | tf_op jit(solution)/shard_map/pallas_call | solution.py:523

commit v2 on v1

--- a/solution.py
+++ b/solution.py
@@ -56,10 +56,10 @@
     k_out, v_out, tg, vg_out,
     vis, vis_all, text, wp, wk, wv, xt, gk, gv, gik, giv, emb, xi, dimg, dg,
     t_send, t_own, t_l1, t_s2, t_l2, i_send, i_own, i_l1, i_s2, i_l2,
-    d_send, d_own, d_l1, d_s2, d_l2, kvt, kvi,
-    st_t, sr_t, st_i, sr_i, sc_t, co_t, sc_i, co_i,
+    d_send, d_own, d_l1, d_s2, d_l2,
+    st_t, sr_t, st_i, sr_i, st_q, sr_q, sc_t, co_t, sc_i, co_i,
     r1k, r1v, s2k, s2v, r2k, r2v, kvb, r3, s4, r4,
-    load_sem, ag_s, ag_r, rs_s, rs_r, st_s, st_r, dv_s, dv_r,
+    load_sem, ag_s, ag_r, rs_s, rs_r, t2_s, t2_r, st_s, st_r, dv_s, dv_r,
     a1_s, a1_r, a2_s, a2_r, b1_s, b1_r, b2_s, b2_r, dt,
 ):
     me_d = lax.axis_index("dp")
@@ -75,6 +75,9 @@
     dv = vis.shape[1]
     d_model = width * mp
     rb = r1k.shape[1]
+    img_rows = mp * rows
+    t_pieces = 2 * slots
+    piece_rows = tokens // t_pieces
 
     def ynext(k):
         return lax.rem(y + k, ycount)
@@ -219,80 +222,93 @@
             total = total + l2[k].astype(F32)
         return total
 
+    def text_piece(p, k):
+        at = pl.ds(p * piece_rows, piece_rows)
+        return remote(
+            t_s2.at[k, at], t_l2.at[k, at], t2_s.at[k, p], t2_r.at[k, p], (me_d, ynext(k) * 2 + core)
+        )
+
+    def text_go(p):
+        for k in range(ycount - 1, 0, -1):
+            copy = text_piece(p, k)
+            copy.start()
+            sends.append(copy)
+
     def stats_send(n, st, sr):
         for k in range(1, mp):
             send(st, sr.at[k], st_s.at[n, k], st_r.at[n, k], (me_d, lax.rem(me + k, mp)))
 
-    def stats_end(n, st, sr, sc, co, keep):
+    def stats_total(n, st, sr):
         total = st[...]
         for k in range(1, mp):
             arrived(sr.at[k], st_s.at[n, k], st_r.at[n, k])
             total = total + sr[k]
-        sq, inner = to_columns(total)
-        scale = lax.rsqrt(sq / d_model + 1e-05)
-        sc[...] = jnp.broadcast_to(scale * keep, sc.shape)
-        co[...] = jnp.broadcast_to(scale * scale * scale * (inner / d_model) * keep, co.shape)
+        return to_columns(total)
+
+    def fold(p):
+        total = p[:, :128]
+        for n in range(1, p.shape[1] // 128):
+            total = total + p[:, n * 128:(n + 1) * 128]
+        return total
 
     loads[3].wait()
     tf = text[...].astype(F32)
-    sq_t = jnp.sum(tf * tf, axis=1, keepdims=True)
+    sc_t[...] = fold(tf * tf)
     xt[...] = (tf * gain[...]).astype(BF16)
     loads[4].wait()
     loads[5].wait()
     stage(xt, 0, t_send, t_own, t_l1)
+    level_two(0, t_own, t_l1, t_s2, t_l2)
     gather_relay(0, vis_block)
-    level_two(0, t_own, t_l1, t_s2, t_l2)
+    loads[7].wait()
+    loads[8].wait()
+
+    @pl.loop(1, dp)
+    def _(k):
+        for which, dst in ((0, r1k), (1, r1v)):
+            block = dst.at[pl.ds(dprev(k) * slots, slots)]
+            remote(block, block, a1_s.at[which, k], a1_r.at[which, k], (me_d, partner)).wait_recv()
+
+    @pl.loop(0, dp)
+    def _(i):
+        s2k[i] = r1k[slot_ref[i]]
+        s2v[i] = r1v[slot_ref[i]]
+
+    r2k[me_d] = s2k[me_d]
+    r2v[me_d] = s2v[me_d]
+
+    def a2(k, which):
+        src, dst = ((s2k, r2k), (s2v, r2v))[which]
+        return remote(
+            src.at[dnext(k)], dst.at[me_d], a2_s.at[which, k], a2_r.at[which, k], (dnext(k), me)
+        )
+
+    @pl.loop(1, dp)
+    def _(k):
+        a2(k, 0).start()
+        a2(k, 1).start()
 
     gather_finish(0, vis_block)
     loads[6].wait()
     step = 256
-    dimg_rows = mp * rows
-
-
-    def project(j, acc):
+
+    sc_i[...] = jnp.zeros(sc_i.shape, F32)
+
+    def project(j, _):
         cs = pl.ds(pl.multiple_of(j * step, step), step)
         e = jnp.concatenate([vis_all[m] for m in range(mp)], axis=0)
         e = jnp.dot(e, wp[:, cs], preferred_element_type=F32).astype(BF16)
         emb[:, cs] = e
         ef = e.astype(F32)
         xi[:, cs] = (ef * gain[:, cs]).astype(BF16)
-        return acc + jnp.sum(ef * ef, axis=1, keepdims=True)
-
-    half = width // step // 2
-    sq_i = lax.fori_loop(0, half, project, jnp.zeros((dimg_rows, 1), F32))
-
-    loads[7].wait()
-    loads[8].wait()
-
-    @pl.loop(1, dp)
-    def _(k):
-        for which, dst in ((0, r1k), (1, r1v)):
-            block = dst.at[pl.ds(dprev(k) * slots, slots)]
-            remote(block, block, a1_s.at[which, k], a1_r.at[which, k], (me_d, partner)).wait_recv()
-
-    @pl.loop(0, dp)
-    def _(i):
-        s2k[i] = r1k[slot_ref[i]]
-        s2v[i] = r1v[slot_ref[i]]
-
-    r2k[me_d] = s2k[me_d]
-    r2v[me_d] = s2v[me_d]
-
-    def a2(k, which):
-        src, dst = ((s2k, r2k), (s2v, r2v))[which]
-        return remote(
-            src.at[dnext(k)], dst.at[me_d], a2_s.at[which, k], a2_r.at[which, k], (dnext(k), me)
-        )
-
-    @pl.loop(1, dp)
-    def _(k):
-        a2(k, 0).start()
-        a2(k, 1).start()
-
-    sq_i = lax.fori_loop(half, width // step, project, sq_i)
+        sc_i[...] += fold(ef * ef)
+        return 0
+
+    lax.fori_loop(0, width // step, project, 0)
+    zero = jnp.zeros((img_rows, 1), F32)
+    st_q[...] = to_rows(jnp.sum(sc_i[...], axis=1, keepdims=True), zero)
+    stats_send(2, st_q, sr_q)
     stage(xi, 1, i_send, i_own, i_l1)
-    level_two(1, i_own, i_l1, i_s2, i_l2)
-    level_go(1, i_s2, i_l2)
 
     @pl.loop(1, dp)
     def _(k):
@@ -306,40 +322,55 @@
     giv[:, col(me)] = own_v.astype(BF16)
     gather_start(3, gik_block)
     gather_start(4, giv_block)
-    level_go(0, t_s2, t_l2)
+    level_two(1, i_own, i_l1, i_s2, i_l2)
+    level_go(1, i_s2, i_l2)
     gather_relay(1, gk_block)
     gather_relay(2, gv_block)
     gather_finish(1, gk_block)
     gather_finish(2, gv_block)
+    co_t[...] = jnp.zeros(co_t.shape, F32)
 
     def text_product(j, _):
         cs = pl.ds(pl.multiple_of(j * step, step), step)
-        dt[:, cs] = (nt(gk[...], wk[cs, :]) + nt(gv[...], wv[cs, :])) * gain[:, cs]
+        d = (nt(gk[...], wk[cs, :]) + nt(gv[...], wv[cs, :])) * gain[:, cs]
+        dt[:, cs] = d
+        co_t[...] += fold(d * text[:, cs].astype(F32))
         return 0
 
     lax.fori_loop(0, width // step, text_product, 0)
-
-    total = level_end(1, i_own, i_l1, i_l2)
-    kvi[...] = total
-    inner = jnp.sum(
-        total[:, :kvd] * gik[:, col(me)].astype(F32) + total[:, kvd:] * giv[:, col(me)].astype(F32),
-        axis=1, keepdims=True,
+    st_t[...] = to_rows(
+        jnp.sum(sc_t[...], axis=1, keepdims=True), jnp.sum(co_t[...], axis=1, keepdims=True)
     )
-    st_i[...] = to_rows(sq_i, inner)
-    stats_send(1, st_i, sr_i)
+    stats_send(0, st_t, sr_t)
     gather_relay(3, gik_block)
     gather_relay(4, giv_block)
     gather_finish(3, gik_block)
     gather_finish(4, giv_block)
+    co_i[...] = jnp.zeros(co_i.shape, F32)
 
     def image_back(j, _):
         cs = pl.ds(pl.multiple_of(j * step, step), step)
-        dg[:, cs] = (nt(gik[...], wk[cs, :]) + nt(giv[...], wv[cs, :])) * gain[:, cs]
+        d = (nt(gik[...], wk[cs, :]) + nt(giv[...], wv[cs, :])) * gain[:, cs]
+        dg[:, cs] = d
+        co_i[...] += fold(d * emb[:, cs].astype(F32))
         return 0
 
     lax.fori_loop(0, width // step, image_back, 0)
-    stats_end(1, st_i, sr_i, sc_i, co_i, 1.0)
-    kvb[...] = (kvi[...] * sc_i[:, 0:1]).reshape(dp, rb, 2 * kvd).astype(BF16)
+    st_i[...] = to_rows(zero, jnp.sum(co_i[...], axis=1, keepdims=True))
+    stats_send(1, st_i, sr_i)
+    early = t_pieces // 2
+    for p in range(early):
+        text_go(p)
+    sq_i, _ = stats_total(2, st_q, sr_q)
+    scale_i = lax.rsqrt(sq_i / d_model + 1e-05)
+    sc_i[...] = jnp.broadcast_to(scale_i, sc_i.shape)
+    sq_t, inner_t = stats_total(0, st_t, sr_t)
+    keep = jnp.concatenate([jnp.full((PATCH, 1), 1.0, F32) * (1.0 - filled(s)) for s in range(slots)], axis=0)
+    scale_t = lax.rsqrt(sq_t / d_model + 1e-05)
+    sc_t[...] = jnp.broadcast_to(scale_t * keep, sc_t.shape)
+    co_t[...] = jnp.broadcast_to(scale_t * scale_t * scale_t * (inner_t / d_model) * keep, co_t.shape)
+    total = level_end(1, i_own, i_l1, i_l2)
+    kvb[...] = (total * sc_i[:, 0:1]).reshape(dp, rb, 2 * kvd).astype(BF16)
     r3[me_d] = kvb[me_d]
 
     def b1(k):
@@ -348,6 +379,18 @@
     @pl.loop(1, dp)
     def _(k):
         b1(k).start()
+
+
+    def text_back(j, _):
+        cs = pl.ds(pl.multiple_of(j * step, step), step)
+        d = sc_t[:, 0:1] * dt[:, cs] - text[:, cs].astype(F32) * co_t[:, 0:1]
+        tg[:, cs] = d.astype(BF16)
+        return 0
+
+    lax.fori_loop(0, width // step, text_back, 0)
+    _, inner_i = stats_total(1, st_i, sr_i)
+    scale_i = sc_i[:, 0:1]
+    co_i[...] = jnp.broadcast_to(scale_i * scale_i * scale_i * (inner_i / d_model), co_i.shape)
 
     def image_end(j, _):
         cs = pl.ds(pl.multiple_of(j * step, step), step)
@@ -356,7 +399,6 @@
         return 0
 
     lax.fori_loop(0, width // step, image_end, 0)
-
     pieces = d_send.shape[0]
     span = dv // pieces
 
@@ -403,26 +445,10 @@
                 b2(k).start()
 
     vis_two(pieces - 1)
-
-    total = level_end(0, t_own, t_l1, t_l2)
-    kvt[...] = total
-    inner = jnp.sum(
-        total[:, :kvd] * gk[:, col(me)].astype(F32) + total[:, kvd:] * gv[:, col(me)].astype(F32),
-        axis=1, keepdims=True,
-    )
-    st_t[...] = to_rows(sq_t, inner)
-    stats_send(0, st_t, sr_t)
-    keep = jnp.concatenate([jnp.full((PATCH, 1), 1.0, F32) * (1.0 - filled(s)) for s in range(slots)], axis=0)
-    stats_end(0, st_t, sr_t, sc_t, co_t, keep)
-
-    def text_back(j, _):
-        cs = pl.ds(pl.multiple_of(j * step, step), step)
-        d = sc_t[:, 0:1] * dt[:, cs] - text[:, cs].astype(F32) * co_t[:, 0:1]
-        tg[:, cs] = d.astype(BF16)
-        return 0
-
-    lax.fori_loop(0, width // step, text_back, 0)
-
+    for p in range(early, t_pieces):
+        text_go(p)
+    vf = vis[...].astype(F32)
+    vscale = lax.rsqrt(jnp.mean(vf * vf, axis=1, keepdims=True) + 1e-06)
     hs = []
     for j in range(pieces):
         d = d_own[j, y] + d_l1[j, y].astype(F32)
@@ -430,8 +456,6 @@
             arrived(d_l2.at[j, k], dv_s.at[1, j, k], dv_r.at[1, j, k])
             d = d + d_l2[j, k].astype(F32)
         hs.append(d.astype(BF16).astype(F32))
-    vf = vis[...].astype(F32)
-    vscale = lax.rsqrt(jnp.mean(vf * vf, axis=1, keepdims=True) + 1e-06)
     h = jnp.concatenate(hs, axis=1) * gain_row(vgain)
     v_inner = jnp.mean(h * vf, axis=1, keepdims=True)
     vg_out[...] = (vscale * h - vf * vscale * vscale * vscale * v_inner).astype(BF16)
@@ -441,12 +465,19 @@
         block = r4.at[:, dprev(k)]
         remote(block, block, b2_s.at[k], b2_r.at[k], (me_d, partner)).wait_recv()
 
-    for s in range(slots):
-        at = pl.ds(s * PATCH, PATCH)
-        out = kvt[at, :] * sc_t[at, 0:1] + r4[s].astype(F32).reshape(PATCH, 2 * kvd) * filled(s)
+    arrived(t_l1.at[y], rs_s.at[0, 0, 0], rs_r.at[0, 0, 0])
+    for p in range(t_pieces):
+        at = pl.ds(p * piece_rows, piece_rows)
+        total = t_own[y, at, :] + t_l1[y, at, :].astype(F32)
+        for k in range(1, ycount):
+            text_piece(p, k).wait_recv()
+            total = total + t_l2[k, at, :].astype(F32)
+        s, half = p // 2, p % 2
+        group = pl.ds(half * (dp // 2), dp // 2)
+        placed = r4[s, group].astype(F32).reshape(piece_rows, 2 * kvd)
+        out = total * sc_t[at, 0:1] + placed * filled(s)
         k_out[at, :] = out[:, :kvd].astype(BF16)
         v_out[at, :] = out[:, kvd:].astype(BF16)
-
     for copy in sends:
         copy.wait_send()
 
@@ -491,15 +522,15 @@
     scratch += [
         V((pieces, ys, rows, span), BF16), V((pieces, ys, rows, span), F32), V((pieces, ys, rows, span), BF16),
         V((pieces, ys, rows, span), BF16), V((pieces, ys, rows, span), BF16),
-        V((tokens, 2 * kvd), F32), V((img, 2 * kvd), F32),
         V((8, tokens), F32), V((mp, 8, tokens), F32), V((8, img), F32), V((mp, 8, img), F32),
+        V((8, img), F32), V((mp, 8, img), F32),
         V((tokens, 128), F32), V((tokens, 128), F32), V((img, 128), F32), V((img, 128), F32),
         V((dp * slots, rb, kvd), BF16), V((dp * slots, rb, kvd), BF16),
         V((dp, rb, kvd), BF16), V((dp, rb, kvd), BF16), V((dp, rb, kvd), BF16), V((dp, rb, kvd), BF16),
         V((dp, rb, 2 * kvd), BF16), V((dp, rb, 2 * kvd), BF16),
         V((dp, slots, rb, 2 * kvd), BF16), V((slots, dp, rb, 2 * kvd), BF16),
         DMA((9,)), DMA((5, 2, ys)), DMA((5, 2, ys)), DMA((2, 2, ys)), DMA((2, 2, ys)),
-        DMA((2, mp)), DMA((2, mp)), DMA((2, pieces, ys)), DMA((2, pieces, ys)),
+        DMA((ys, 2 * slots)), DMA((ys, 2 * slots)), DMA((3, mp)), DMA((3, mp)), DMA((2, pieces, ys)), DMA((2, pieces, ys)),
         DMA((2, dp)), DMA((2, dp)), DMA((2, dp)), DMA((2, dp)),
         DMA((dp,)), DMA((dp,)), DMA((dp,)), DMA((dp,)), V((tokens, width), F32),
     ]

time: 76.7 us -> 69.8 us (0.910)
  Pallas kernels: 75.7 us -> 68.8 us
    pallas_call x1, Pallas kernels: 74.1 us -> 67.1 us  [shards(): pl.pallas_call(functools.partial(kernel, dp, mp), out_shape=tuple((V(shap...]
where the time goes in v2:
time: 69.8 us; the launch traced here: 69.6 us
  Pallas kernels  68.8 us (99%)
  between operations  0.8 us (1%)
    pallas_call x1, Pallas kernels, shards(): pl.pallas_call(functools.partial(kernel, dp, mp), out_shape=tuple((V(shap...  67.1 us
    pallas_call x1, Pallas kernels, shards(): pl.pallas_call(write_out, out_shape=tuple((jax.ShapeDtypeStruct(shape, BF...  1.65 us

profile of v2, /device:TPU:0, one launch (start us, length us, event | category | flops | bytes accessed | tf_op | source)
XLA Modules:
  0.0 69.6 jit_solution(4788930224128420154)
XLA Ops:
  0.6 67.1 %shard_map.129 = (bf16[512,256]{1,0:T(8,128)(2,1)S(1)}, bf16[512,256]{1,0:T(8,128)(2,1)S(1)}, bf16[512,2048]{1,0:T(8,128)(2,1)S(1)}, bf16[64,3200]{1,0:T(8,128)(2,1)S(1)}) custom-call(s32[8]{0:T(128)} %slot_ref.1, bf16[64,3200]{1,0:T(8,128)(2,1)} %vision_h.1, f32[25,128]{1,0:T(8,128)} %bitcast.6, bf16[512,2048]{1,0:T(8,128)(2,1)} %text_h.1, ...), custom_call_target="tpu_custom_call" | custom-call | tf_op jit(solution)/shard_map/pallas_call | solution.py:540
  67.8 1.7 %shard_map.130 = (bf16[512,256]{1,0:T(8,128)(2,1)}, bf16[512,256]{1,0:T(8,128)(2,1)}, bf16[512,2048]{1,0:T(8,128)(2,1)}, bf16[64,3200]{1,0:T(8,128)(2,1)}) custom-call(bf16[512,256]{1,0:T(8,128)(2,1)S(1)} %get-tuple-element.8.refs_0_, bf16[512,256]{1,0:T(8,128)(2,1)S(1)} %get-tuple-element.9.refs_1_, bf16[512,2048]{1,0:T(8,128)(2,1)S(1)} %get-tuple-element.10.refs_2_, ...), custom_call_target="tpu_custom_call" | custom-call | tf_op jit(solution)/shard_map/pallas_call | solution.py:554

commit v3 on v2

--- a/solution.py
+++ b/solution.py
@@ -58,9 +58,11 @@
     t_send, t_own, t_l1, t_s2, t_l2, i_send, i_own, i_l1, i_s2, i_l2,
     d_send, d_own, d_l1, d_s2, d_l2,
     st_t, sr_t, st_i, sr_i, st_q, sr_q, sc_t, co_t, sc_i, co_i,
+    kgs, vgs, kb_send, kb_y, kbr, tb_send, tb_recv, tb_sel, tb_y,
     r1k, r1v, s2k, s2v, r2k, r2v, kvb, r3, s4, r4,
     load_sem, ag_s, ag_r, rs_s, rs_r, t2_s, t2_r, st_s, st_r, dv_s, dv_r,
-    a1_s, a1_r, a2_s, a2_r, b1_s, b1_r, b2_s, b2_r, dt,
+    a1_s, a1_r, a2_s, a2_r, b1_s, b1_r, b2_s, b2_r, kby_s, kby_r, kbz_s, kbz_r, kbp_s, kbp_r,
+    tbz_s, tbz_r, tby_s, tby_r, dt,
 ):
     me_d = lax.axis_index("dp")
     me = lax.axis_index("mp")
@@ -68,16 +70,16 @@
     core = lax.rem(me, 2)
     y = lax.div(me, 2)
     partner = y * 2 + (1 - core)
-    tokens, width = text.shape
-    slots = tokens // PATCH
+    slots, _, width = text.shape
+    tokens = slots * PATCH
     kvd = gk.shape[1] // mp
     rows = vis.shape[0]
     dv = vis.shape[1]
     d_model = width * mp
     rb = r1k.shape[1]
     img_rows = mp * rows
-    t_pieces = 2 * slots
-    piece_rows = tokens // t_pieces
+    t_pieces = 2
+    piece_rows = PATCH // t_pieces
 
     def ynext(k):
         return lax.rem(y + k, ycount)
@@ -100,11 +102,28 @@
             found = jnp.where(slot_ref[i] == slot, jnp.int32(i), found)
         return found
 
-    def filled(s):
+    def holds(s):
         found = jnp.int32(0)
         for i in range(dp):
             found = jnp.where(slot_ref[i] == me_d * slots + s, jnp.int32(1), found)
-        return found.astype(F32)
+        return found
+
+    first_holds, second_holds = holds(0), holds(1)
+    turned = first_holds * (1 - second_holds)
+    slot_at = (turned, 1 - turned)
+    place_of = (turned, 1 - turned)
+    filled = (first_holds.astype(F32), second_holds.astype(F32))
+    keeps = (1.0 - filled[0] * filled[1], (1.0 - filled[0]) * (1.0 - filled[1]))
+
+    def bare(d, found):
+        used = jnp.int32(0)
+        for i in range(dp):
+            used = jnp.where(lax.div(slot_ref[i], jnp.int32(slots)) == d, jnp.int32(1), used)
+        return jnp.where(used == 0, d, found)
+
+    lone = lax.fori_loop(0, dp, bare, jnp.int32(0))
+    lone_slot = lone * slots + 1
+    at_lone = keeps[1]
 
     sends = []
 
@@ -114,7 +133,7 @@
         sends.append(copy)
 
     loads = [
-        (vision_h, vis), (kg_h, gk.at[:, col(me)]), (vg_h, gv.at[:, col(me)]),
+        (vision_h, vis), (kg_h, kgs), (vg_h, vgs),
         (text_h, text), (wk_h, wk), (wv_h, wv), (wp_h, wp),
         (kg4.at[:, me_d], r1k.at[pl.ds(me_d * slots, slots)]),
         (vg4.at[:, me_d], r1v.at[pl.ds(me_d * slots, slots)]),
@@ -183,26 +202,67 @@
 
     loads[1].wait()
     loads[2].wait()
-    gather_start(1, gk_block)
-    gather_start(2, gv_block)
-
-    def stage(x, n, psend, own, l1):
-        def chunk(m):
-            k_part = jnp.dot(x[...], wk[:, col(m)], preferred_element_type=F32)
-            v_part = jnp.dot(x[...], wv[:, col(m)], preferred_element_type=F32)
-            return k_part, v_part
-
+    for p in range(slots):
+        gk[p * PATCH:(p + 1) * PATCH, col(me)] = kgs[slot_at[p]]
+        gv[p * PATCH:(p + 1) * PATCH, col(me)] = vgs[slot_at[p]]
+    first_rows = pl.ds(0, PATCH)
+    later_rows = pl.ds(PATCH, PATCH)
+    gka_block = lambda m: gk.at[first_rows, col(m)]
+    gva_block = lambda m: gv.at[first_rows, col(m)]
+
+    def pair_start(g, block, whole):
+        for k in range(1, ycount):
+            send(block(me), block(me), ag_s.at[g, 0, k], ag_r.at[g, 0, k], (me_d, ynext(k) * 2 + core))
+        send(whole(me), whole(me), ag_s.at[g, 0, 0], ag_r.at[g, 0, 0], (me_d, partner))
+
+    def near_finish(g, block):
+        arrived(block(partner), ag_s.at[g, 0, 0], ag_r.at[g, 0, 0])
+
+    def far_finish(g, block):
+        for k in range(1, ycount):
+            arrived(block(yprev(k) * 2 + 1 - core), ag_s.at[g, 1, k], ag_r.at[g, 1, k])
+
+    def heads(yk):
+        return pl.ds(pl.multiple_of(yk * 2 * kvd, 2 * kvd), 2 * kvd)
+
+    def products(keys, values, at, cs, yk):
+        at_heads = heads(yk)
+        return nt(keys[at, at_heads], wk[cs, at_heads]) + nt(values[at, at_heads], wv[cs, at_heads])
+
+    def far_products(keys, values, at, cs):
+        total = products(keys, values, at, cs, ynext(1))
+        for k in range(2, ycount):
+            total = total + products(keys, values, at, cs, ynext(k))
+        return total
+
+    step = 256
+    every = pl.ds(0, tokens)
+    image_rows = pl.ds(0, img_rows)
+
+    pair_start(1, gka_block, gk_block)
+    pair_start(2, gva_block, gv_block)
+
+    def chunk(x, m):
+        k_part = jnp.dot(x[...], wk[:, col(m)], preferred_element_type=F32)
+        v_part = jnp.dot(x[...], wv[:, col(m)], preferred_element_type=F32)
+        return k_part, v_part
+
+    def stage_send(x, n, psend, l1):
         for k in range(ycount):
             yk = ynext(k)
-            k_part, v_part = chunk(yk * 2 + 1 - core)
-            psend[yk, :, :kvd] = k_part.astype(BF16)
-            psend[yk, :, kvd:] = v_part.astype(BF16)
+            k_part, v_part = chunk(x, yk * 2 + 1 - core)
+            shape = psend.shape[1:-1] + (kvd,)
+            psend[yk, ..., :kvd] = k_part.astype(BF16).reshape(shape)
+            psend[yk, ..., kvd:] = v_part.astype(BF16).reshape(shape)
             send(psend.at[yk], l1.at[yk], rs_s.at[n, 0, k], rs_r.at[n, 0, k], (me_d, partner))
+
+    def stage_own(x, own):
         for k in range(ycount):
             yk = ynext(k)
-            k_part, v_part = chunk(yk * 2 + core)
-            own[yk, :, :kvd] = k_part
-            own[yk, :, kvd:] = v_part
+            k_part, v_part = chunk(x, yk * 2 + core)
+            shape = own.shape[1:-1] + (kvd,)
+            own[yk, ..., :kvd] = k_part.reshape(shape)
+            own[yk, ..., kvd:] = v_part.reshape(shape)
 
     def level_two(n, own, l1, s2, l2):
         for k in range(ycount - 1, 0, -1):
@@ -252,13 +312,31 @@
         return total
 
     loads[3].wait()
-    tf = text[...].astype(F32)
-    sc_t[...] = fold(tf * tf)
-    xt[...] = (tf * gain[...]).astype(BF16)
+    for p in range(slots):
+        tf = text[slot_at[p]].astype(F32)
+        sc_t[p] = fold(tf * tf)
+        xt[p * PATCH:(p + 1) * PATCH, :] = (tf * gain[...]).astype(BF16)
     loads[4].wait()
     loads[5].wait()
-    stage(xt, 0, t_send, t_own, t_l1)
-    level_two(0, t_own, t_l1, t_s2, t_l2)
+    stage_send(xt, 0, t_send, t_l1)
+    stage_own(xt, t_own)
+    for k in range(ycount - 1, 0, -1):
+        yk = ynext(k)
+        arrived(t_l1.at[yk], rs_s.at[0, 0, k], rs_r.at[0, 0, k])
+        t_s2[k] = (t_own[yk, 0] + t_l1[yk, 0].astype(F32)).astype(BF16)
+        rest = t_own[yk, 1] + t_l1[yk, 1].astype(F32)
+        tb_send[:, k - 1] = rest.reshape(dp, rb, 2 * kvd).astype(BF16)
+    tb_recv[me_d] = tb_send[me_d]
+    near_finish(1, gk_block)
+    near_finish(2, gv_block)
+
+    def text_near(j, _):
+        cs = pl.ds(pl.multiple_of(j * step, step), step)
+        dt[:, :, cs] = products(gk, gv, every, cs, y).reshape(slots, PATCH, step)
+        return 0
+
+    lax.fori_loop(0, width // step, text_near, 0)
+    co_t[...] = jnp.zeros(co_t.shape, F32)
     gather_relay(0, vis_block)
     loads[7].wait()
     loads[8].wait()
@@ -288,9 +366,12 @@
         a2(k, 0).start()
         a2(k, 1).start()
 
+    kb_send[0] = r1k[lone_slot]
+    kb_send[1] = r1v[lone_slot]
+    for k in range(1, ycount):
+        send(kb_send, kb_y.at[k - 1], kby_s.at[k], kby_r.at[k], (me_d, ynext(k) * 2 + core))
     gather_finish(0, vis_block)
     loads[6].wait()
-    step = 256
 
     sc_i[...] = jnp.zeros(sc_i.shape, F32)
 
@@ -305,10 +386,30 @@
         return 0
 
     lax.fori_loop(0, width // step, project, 0)
+    for k in range(1, ycount):
+        arrived(kb_y.at[k - 1], kby_s.at[k], kby_r.at[k])
+    kbr[me_d] = kb_y[...]
+
+    def kbz(k):
+        return remote(kb_y, kbr.at[me_d], kbz_s.at[k], kbz_r.at[k], (dnext(k), me))
+
+    def tbz(k):
+        return remote(tb_send.at[dnext(k)], tb_recv.at[me_d], tbz_s.at[k], tbz_r.at[k], (dnext(k), me))
+
+    @pl.loop(1, dp)
+    def _(k):
+        kbz(k).start()
+
+    @pl.loop(1, dp)
+    def _(k):
+        tbz(k).start()
+
+    gather_relay(1, gka_block)
+    gather_relay(2, gva_block)
     zero = jnp.zeros((img_rows, 1), F32)
     st_q[...] = to_rows(jnp.sum(sc_i[...], axis=1, keepdims=True), zero)
     stats_send(2, st_q, sr_q)
-    stage(xi, 1, i_send, i_own, i_l1)
+    stage_send(xi, 1, i_send, i_l1)
 
     @pl.loop(1, dp)
     def _(k):
@@ -322,53 +423,87 @@
     giv[:, col(me)] = own_v.astype(BF16)
     gather_start(3, gik_block)
     gather_start(4, giv_block)
+    stage_own(xi, i_own)
     level_two(1, i_own, i_l1, i_s2, i_l2)
     level_go(1, i_s2, i_l2)
-    gather_relay(1, gk_block)
-    gather_relay(2, gv_block)
-    gather_finish(1, gk_block)
-    gather_finish(2, gv_block)
-    co_t[...] = jnp.zeros(co_t.shape, F32)
-
-    def text_product(j, _):
+    far_finish(1, gka_block)
+    far_finish(2, gva_block)
+
+    def text_far(p):
+        rows_p = pl.ds(p * PATCH, PATCH)
+
+        def body(j, _):
+            cs = pl.ds(pl.multiple_of(j * step, step), step)
+            d = (dt[p, :, cs] + far_products(gk, gv, rows_p, cs)) * gain[:, cs]
+            dt[p, :, cs] = d
+            co_t[p] += fold(d * text[slot_at[p], :, cs].astype(F32))
+            return 0
+
+        lax.fori_loop(0, width // step, body, 0)
+
+    text_far(0)
+    near_finish(3, gik_block)
+    near_finish(4, giv_block)
+
+    def image_near(j, _):
         cs = pl.ds(pl.multiple_of(j * step, step), step)
-        d = (nt(gk[...], wk[cs, :]) + nt(gv[...], wv[cs, :])) * gain[:, cs]
-        dt[:, cs] = d
-        co_t[...] += fold(d * text[:, cs].astype(F32))
+        dg[:, cs] = products(gik, giv, image_rows, cs, y)
         return 0
 
-    lax.fori_loop(0, width // step, text_product, 0)
+    lax.fori_loop(0, width // step, image_near, 0)
+    co_i[...] = jnp.zeros(co_i.shape, F32)
+
+    @pl.loop(1, dp)
+    def _(k):
+        block = kbr.at[dprev(k)]
+        remote(block, block, kbz_s.at[k], kbz_r.at[k], (me_d, partner)).wait_recv()
+
+    for k in range(1, ycount):
+        m = yprev(k) * 2 + core
+        for which, g in ((0, gk), (1, gv)):
+            g[later_rows, col(m)] = kbr[:, k - 1, which].astype(F32).reshape(PATCH, kvd).astype(BF16)
+            send(
+                g.at[later_rows, col(m)], g.at[later_rows, col(m)], kbp_s.at[which, k], kbp_r.at[which, k],
+                (me_d, partner),
+            )
+    gather_relay(3, gik_block)
+    gather_relay(4, giv_block)
+    for k in range(1, ycount):
+        for which, g in ((0, gk), (1, gv)):
+            arrived(g.at[later_rows, col(yprev(k) * 2 + 1 - core)], kbp_s.at[which, k], kbp_r.at[which, k])
+    text_far(1)
     st_t[...] = to_rows(
-        jnp.sum(sc_t[...], axis=1, keepdims=True), jnp.sum(co_t[...], axis=1, keepdims=True)
+        jnp.sum(sc_t[...].reshape(tokens, 128), axis=1, keepdims=True),
+        jnp.sum(co_t[...].reshape(tokens, 128), axis=1, keepdims=True),
     )
     stats_send(0, st_t, sr_t)
-    gather_relay(3, gik_block)
-    gather_relay(4, giv_block)
-    gather_finish(3, gik_block)
-    gather_finish(4, giv_block)
-    co_i[...] = jnp.zeros(co_i.shape, F32)
-
-    def image_back(j, _):
+    far_finish(3, gik_block)
+    far_finish(4, giv_block)
+
+    def image_far(j, _):
         cs = pl.ds(pl.multiple_of(j * step, step), step)
-        d = (nt(gik[...], wk[cs, :]) + nt(giv[...], wv[cs, :])) * gain[:, cs]
+        d = (dg[:, cs] + far_products(gik, giv, image_rows, cs)) * gain[:, cs]
         dg[:, cs] = d
         co_i[...] += fold(d * emb[:, cs].astype(F32))
         return 0
 
-    lax.fori_loop(0, width // step, image_back, 0)
+    lax.fori_loop(0, width // step, image_far, 0)
     st_i[...] = to_rows(zero, jnp.sum(co_i[...], axis=1, keepdims=True))
     stats_send(1, st_i, sr_i)
-    early = t_pieces // 2
-    for p in range(early):
+
+    @pl.loop(1, dp)
+    def _(k):
+        block = tb_recv.at[dprev(k)]
+        remote(block, block, tbz_s.at[k], tbz_r.at[k], (me_d, partner)).wait_recv()
+
+    tb_sel[...] = tb_recv[lone]
+    for k in range(1, ycount):
+        send(tb_sel.at[k - 1], tb_y.at[k - 1], tby_s.at[k], tby_r.at[k], (me_d, ynext(k) * 2 + core))
+    for p in range(t_pieces):
         text_go(p)
     sq_i, _ = stats_total(2, st_q, sr_q)
     scale_i = lax.rsqrt(sq_i / d_model + 1e-05)
     sc_i[...] = jnp.broadcast_to(scale_i, sc_i.shape)
-    sq_t, inner_t = stats_total(0, st_t, sr_t)
-    keep = jnp.concatenate([jnp.full((PATCH, 1), 1.0, F32) * (1.0 - filled(s)) for s in range(slots)], axis=0)
-    scale_t = lax.rsqrt(sq_t / d_model + 1e-05)
-    sc_t[...] = jnp.broadcast_to(scale_t * keep, sc_t.shape)
-    co_t[...] = jnp.broadcast_to(scale_t * scale_t * scale_t * (inner_t / d_model) * keep, co_t.shape)
     total = level_end(1, i_own, i_l1, i_l2)
     kvb[...] = (total * sc_i[:, 0:1]).reshape(dp, rb, 2 * kvd).astype(BF16)
     r3[me_d] = kvb[me_d]
@@ -380,11 +515,20 @@
     def _(k):
         b1(k).start()
 
+    sq_t, inner_t = stats_total(0, st_t, sr_t)
+    keep = jnp.concatenate([jnp.full((PATCH, 1), 1.0, F32) * keeps[p] for p in range(slots)], axis=0)
+    scale_t = lax.rsqrt(sq_t / d_model + 1e-05)
+    sc_t[...] = jnp.broadcast_to(scale_t * keep, (tokens, 128)).reshape(sc_t.shape)
+    co_t[...] = jnp.broadcast_to(
+        scale_t * scale_t * scale_t * (inner_t / d_model) * keep, (tokens, 128)
+    ).reshape(co_t.shape)
 
     def text_back(j, _):
         cs = pl.ds(pl.multiple_of(j * step, step), step)
-        d = sc_t[:, 0:1] * dt[:, cs] - text[:, cs].astype(F32) * co_t[:, 0:1]
-        tg[:, cs] = d.astype(BF16)
+        for s in range(slots):
+            at = place_of[s]
+            d = sc_t[at][:, 0:1] * dt[at, :, cs] - text[s, :, cs].astype(F32) * co_t[at][:, 0:1]
+            tg[s * PATCH:(s + 1) * PATCH, cs] = d.astype(BF16)
         return 0
 
     lax.fori_loop(0, width // step, text_back, 0)
@@ -432,10 +576,17 @@
                 block = r3.at[dprev(k)]
                 remote(block, block, b1_s.at[k], b1_r.at[k], (me_d, partner)).wait_recv()
 
+            extra = jnp.zeros((rb, 2 * kvd), F32)
+            for k in range(1, ycount):
+                arrived(tb_y.at[k - 1], tby_s.at[k], tby_r.at[k])
+                extra = extra + tb_y[k - 1].astype(F32)
+            r3[dp] = extra.astype(BF16)
+
             @pl.loop(0, dp)
             def _(d):
                 for s in range(slots):
-                    s4[d, s] = r3[owner_of(d * slots + s)]
+                    slot = d * slots + s
+                    s4[d, s] = r3[jnp.where(slot == lone_slot, jnp.int32(dp), owner_of(slot))]
 
             for s in range(slots):
                 r4[s, me_d] = s4[me_d, s]
@@ -445,8 +596,6 @@
                 b2(k).start()
 
     vis_two(pieces - 1)
-    for p in range(early, t_pieces):
-        text_go(p)
     vf = vis[...].astype(F32)
     vscale = lax.rsqrt(jnp.mean(vf * vf, axis=1, keepdims=True) + 1e-06)
     hs = []
@@ -467,17 +616,20 @@
 
     arrived(t_l1.at[y], rs_s.at[0, 0, 0], rs_r.at[0, 0, 0])
     for p in range(t_pieces):
-        at = pl.ds(p * piece_rows, piece_rows)
-        total = t_own[y, at, :] + t_l1[y, at, :].astype(F32)
         for k in range(1, ycount):
             text_piece(p, k).wait_recv()
-            total = total + t_l2[k, at, :].astype(F32)
-        s, half = p // 2, p % 2
-        group = pl.ds(half * (dp // 2), dp // 2)
-        placed = r4[s, group].astype(F32).reshape(piece_rows, 2 * kvd)
-        out = total * sc_t[at, 0:1] + placed * filled(s)
-        k_out[at, :] = out[:, :kvd].astype(BF16)
-        v_out[at, :] = out[:, kvd:].astype(BF16)
+    direct = t_l2[1].astype(F32)
+    for k in range(2, ycount):
+        direct = direct + t_l2[k].astype(F32)
+    for s in range(slots):
+        at = place_of[s]
+        is_first = 1.0 - at.astype(F32)
+        placed = r4[s].astype(F32).reshape(PATCH, 2 * kvd)
+        total = t_own[y, at] + t_l1[y, at].astype(F32) + direct * is_first + placed * ((1.0 - is_first) * at_lone)
+        out = total * sc_t[at][:, 0:1] + placed * filled[s]
+        rows_s = pl.ds(s * PATCH, PATCH)
+        k_out[rows_s, :] = out[:, :kvd].astype(BF16)
+        v_out[rows_s, :] = out[:, kvd:].astype(BF16)
     for copy in sends:
         copy.wait_send()
 
@@ -488,6 +640,8 @@
         a2(k, 0).wait_send()
         a2(k, 1).wait_send()
         b1(k).wait_send()
+        kbz(k).wait_send()
+        tbz(k).wait_send()
         b2(k).wait_send()
 
 
@@ -509,30 +663,36 @@
     vmem = pl.BlockSpec(memory_space=pltpu.VMEM)
     smem = pl.BlockSpec(memory_space=pltpu.SMEM)
     scratch = [
-        V((rows, dv), BF16), V((mp, rows, dv), BF16), V((tokens, width), BF16), V((dv, width), BF16),
+        V((rows, dv), BF16), V((mp, rows, dv), BF16), V((slots, PATCH, width), BF16), V((dv, width), BF16),
         V((width, kv), BF16), V((width, kv), BF16), V((tokens, width), BF16),
         V((tokens, kv), BF16), V((tokens, kv), BF16), V((img, kv), BF16), V((img, kv), BF16),
         V((img, width), BF16), V((img, width), BF16), V((img, width), BF16), V((img, width), F32),
     ]
-    for n in (tokens, img):
-        scratch += [
-            V((ys, n, 2 * kvd), BF16), V((ys, n, 2 * kvd), F32), V((ys, n, 2 * kvd), BF16),
-            V((ys, n, 2 * kvd), BF16), V((ys, n, 2 * kvd), BF16),
-        ]
+    t_shape = (ys, slots, PATCH, 2 * kvd)
+    i_shape = (ys, img, 2 * kvd)
+    half = (ys, PATCH, 2 * kvd)
+    scratch += [V(t_shape, BF16), V(t_shape, F32), V(t_shape, BF16), V(half, BF16), V(half, BF16)]
+    scratch += [V(i_shape, BF16), V(i_shape, F32), V(i_shape, BF16), V(i_shape, BF16), V(i_shape, BF16)]
     scratch += [
         V((pieces, ys, rows, span), BF16), V((pieces, ys, rows, span), F32), V((pieces, ys, rows, span), BF16),
         V((pieces, ys, rows, span), BF16), V((pieces, ys, rows, span), BF16),
         V((8, tokens), F32), V((mp, 8, tokens), F32), V((8, img), F32), V((mp, 8, img), F32),
         V((8, img), F32), V((mp, 8, img), F32),
-        V((tokens, 128), F32), V((tokens, 128), F32), V((img, 128), F32), V((img, 128), F32),
+        V((slots, PATCH, 128), F32), V((slots, PATCH, 128), F32), V((img, 128), F32), V((img, 128), F32),
+        V((slots, PATCH, kvd), BF16), V((slots, PATCH, kvd), BF16),
+        V((2, rb, kvd), BF16), V((ys - 1, 2, rb, kvd), BF16), V((dp, ys - 1, 2, rb, kvd), BF16),
+        V((dp, ys - 1, rb, 2 * kvd), BF16), V((dp, ys - 1, rb, 2 * kvd), BF16),
+        V((ys - 1, rb, 2 * kvd), BF16), V((ys - 1, rb, 2 * kvd), BF16),
         V((dp * slots, rb, kvd), BF16), V((dp * slots, rb, kvd), BF16),
         V((dp, rb, kvd), BF16), V((dp, rb, kvd), BF16), V((dp, rb, kvd), BF16), V((dp, rb, kvd), BF16),
-        V((dp, rb, 2 * kvd), BF16), V((dp, rb, 2 * kvd), BF16),
+        V((dp, rb, 2 * kvd), BF16), V((dp + 1, rb, 2 * kvd), BF16),
         V((dp, slots, rb, 2 * kvd), BF16), V((slots, dp, rb, 2 * kvd), BF16),
         DMA((9,)), DMA((5, 2, ys)), DMA((5, 2, ys)), DMA((2, 2, ys)), DMA((2, 2, ys)),
-        DMA((ys, 2 * slots)), DMA((ys, 2 * slots)), DMA((3, mp)), DMA((3, mp)), DMA((2, pieces, ys)), DMA((2, pieces, ys)),
+        DMA((ys, 2)), DMA((ys, 2)), DMA((3, mp)), DMA((3, mp)), DMA((2, pieces, ys)), DMA((2, pieces, ys)),
         DMA((2, dp)), DMA((2, dp)), DMA((2, dp)), DMA((2, dp)),
-        DMA((dp,)), DMA((dp,)), DMA((dp,)), DMA((dp,)), V((tokens, width), F32),
+        DMA((dp,)), DMA((dp,)), DMA((dp,)), DMA((dp,)),
+        DMA((ys,)), DMA((ys,)), DMA((dp,)), DMA((dp,)), DMA((2, ys)), DMA((2, ys)),
+        DMA((dp,)), DMA((dp,)), DMA((ys,)), DMA((ys,)), V((slots, PATCH, width), F32),
     ]
     shapes = ((tokens, kvd), (tokens, kvd), (tokens, width), (rows, dv))
     room = sum(2 * a * b for a, b in shapes)
@@ -547,8 +707,8 @@
             collective_id=0, has_side_effects=True, vmem_limit_bytes=67043328 - room
         ),
     )(
-        image_slot, vision, vision_gain.reshape(-1, lanes), text_embed, w_proj, llm_gain[None, :],
-        w_key, w_value, key_grad, value_grad,
+        image_slot, vision, vision_gain.reshape(-1, lanes), text_embed.reshape(slots, PATCH, width), w_proj,
+        llm_gain[None, :], w_key, w_value, key_grad.reshape(slots, PATCH, kvd), value_grad.reshape(slots, PATCH, kvd),
         key_grad.reshape(slots, dp, rb, kvd), value_grad.reshape(slots, dp, rb, kvd),
     )
     return pl.pallas_call(

time: 69.8 us -> 67.3 us (0.964)
  the two profiles are of different devices: /device:TPU:0 before, /device:TPU:11 now
where the time goes in v3:
time: 67.3 us; the launch traced here: 67.1 us
  Pallas kernels  66.3 us (99%)
  between operations  0.8 us (1%)
    pallas_call x1, Pallas kernels, shards(): pl.pallas_call(functools.partial(kernel, dp, mp), out_shape=tuple((V(shap...  64.6 us
    pallas_call x1, Pallas kernels, shards(): pl.pallas_call(write_out, out_shape=tuple((jax.ShapeDtypeStruct(shape, BF...  1.65 us

profile of v3, /device:TPU:11, one launch (start us, length us, event | category | flops | bytes accessed | tf_op | source)
XLA Modules:
  0.0 67.1 jit_solution(15151183348325788870)
XLA Ops:
  0.6 64.6 %shard_map.129 = (bf16[512,256]{1,0:T(8,128)(2,1)S(1)}, bf16[512,256]{1,0:T(8,128)(2,1)S(1)}, bf16[512,2048]{1,0:T(8,128)(2,1)S(1)}, bf16[64,3200]{1,0:T(8,128)(2,1)S(1)}) custom-call(s32[8]{0:T(128)} %slot_ref.1, bf16[64,3200]{1,0:T(8,128)(2,1)} %vision_h.1, f32[25,128]{1,0:T(8,128)} %bitcast.12, bf16[2,256,2048]{2,1,0:T(8,128)(2,1)} %bitcast.7, ...), custom_call_target="tpu_custom_call" | custom-call | tf_op jit(solution)/shard_map/pallas_call | solution.py:700
  65.2 1.7 %shard_map.130 = (bf16[512,256]{1,0:T(8,128)(2,1)}, bf16[512,256]{1,0:T(8,128)(2,1)}, bf16[512,2048]{1,0:T(8,128)(2,1)}, bf16[64,3200]{1,0:T(8,128)(2,1)}) custom-call(bf16[512,256]{1,0:T(8,128)(2,1)S(1)} %get-tuple-element.8.refs_0_, bf16[512,256]{1,0:T(8,128)(2,1)S(1)} %get-tuple-element.9.refs_1_, bf16[512,2048]{1,0:T(8,128)(2,1)S(1)} %get-tuple-element.10.refs_2_, ...), custom_call_target="tpu_custom_call" | custom-call | tf_op jit(solution)/shard_map/pallas_call | solution.py:714

commit v4 on v3

v4 whole, which is shorter than its diff:
```python
import functools

import jax
import jax.numpy as jnp
from jax import lax
from jax.experimental import pallas as pl
from jax.experimental.pallas import tpu as pltpu
from jax.sharding import PartitionSpec as P

PATCH = 256
F32 = jnp.float32
BF16 = jnp.bfloat16
NT = (((1,), (1,)), ((), ()))
DMA = pltpu.SemaphoreType.DMA


def nt(a, b):
    return lax.dot_general(a, b, NT, preferred_element_type=F32)


def remote(src, dst, send_sem, recv_sem, device):
    return pltpu.make_async_remote_copy(
        src_ref=src, dst_ref=dst, send_sem=send_sem, recv_sem=recv_sem,
        device_id=device, device_id_type=pl.DeviceIdType.MESH,
    )


def to_rows(sq, inner):
    lane = lax.broadcasted_iota(jnp.int32, (sq.shape[0], 128), 1)
    wide = jnp.where(lane == 0, sq, jnp.where(lane == 1, inner, 0.0))
    return jnp.transpose(wide)[:8]


def to_columns(rows):
    wide = jnp.transpose(jnp.concatenate([rows] * 16, axis=0))
    return wide[:, 0:1], wide[:, 1:2]


def gain_row(ref):
    if ref.shape[0] == 1:
        return ref[...]
    return jnp.concatenate([ref[i:i + 1, :] for i in range(ref.shape[0])], axis=1)


def vis_cuts(dv):
    if dv % 128:
        return (0, dv)
    units = dv // 128
    first = max(units // 12, 1)
    cuts = [0, first]
    while cuts[-1] < units:
        cuts.append(min(cuts[-1] + max(units // 5, 1), units))
    return tuple(128 * c for c in cuts)


def write_out(*refs):
    count = (len(refs) - 1) // 2
    copies = [pltpu.make_async_copy(refs[n], refs[count + n], refs[-1].at[n]) for n in range(count)]
    for copy in copies:
        copy.start()
    for copy in copies:
        copy.wait()


def kernel(
    dp, mp, slot_ref, vision_h, vgain, text_h, wp_h, gain, wk_h, wv_h, kg_h, vg_h, kg4, vg4,
    k_out, v_out, tg, vg_out,
    vis, vis_all, text, wp, wk, wv, xt, gk, gv, gik, giv, emb, xi, dimg, dg,
    t_send, t_own, t_l1, t_s2, t_l2, i_send, i_own, i_l1, i_s2, i_l2,
    d_send, d_own, d_l1, d_s2, d_l2,
    st_t, sr_t, st_i, sr_i, st_q, sr_q, sc_t, co_t, sc_i, co_i,
    kgs, vgs, kb_send, kb_y, kbr, tb_send, tb_recv, tb_sel, tb_y,
    r1k, r1v, s2k, s2v, r2k, r2v, kvb, r3, s4, s5, r4,
    load_sem, ag_s, ag_r, rs_s, rs_r, rs1_r, t2_r, st_s, st_r, dv_s, dv_r,
    a1_s, a1_r, a2_s, a2_r, b1_s, b1_r, b2_s, b2_r, b3_s, b3_r, kby_s, kby_r, kbz_s, kbz_r, kbp_s, kbp_r,
    tbz_s, tbz_r, tby_s, tby_r, dt,
):
    me_d = lax.axis_index("dp")
    me = lax.axis_index("mp")
    ycount = mp // 2
    core = lax.rem(me, 2)
    y = lax.div(me, 2)
    partner = y * 2 + (1 - core)
    slots, _, width = text.shape
    tokens = slots * PATCH
    kvd = gk.shape[1] // mp
    rows = vis.shape[0]
    dv = vis.shape[1]
    d_model = width * mp
    rb = r1k.shape[1]
    img_rows = mp * rows
    t_pieces = 2
    piece_rows = PATCH // t_pieces

    def ynext(k):
        return lax.rem(y + k, ycount)

    def yprev(k):
        return lax.rem(y + ycount - k, ycount)

    def dnext(k):
        return lax.rem(me_d + k, dp)

    def dprev(k):
        return lax.rem(me_d + dp - k, dp)

    def col(m):
        return pl.ds(pl.multiple_of(m * kvd, kvd), kvd)

    def is_filled(slot):
        found = jnp.int32(0)
        for i in range(dp):
            found = jnp.where(slot_ref[i] == slot, jnp.int32(1), found)
        return found

    def owner_of(slot):
        found = jnp.int32(0)
        for i in range(dp):
            found = jnp.where(slot_ref[i] == slot, jnp.int32(i), found)
        return found

    def holds(s):
        return is_filled(me_d * slots + s)

    first_holds, second_holds = holds(0), holds(1)
    turned = first_holds * (1 - second_holds)
    slot_at = (turned, 1 - turned)
    place_of = (turned, 1 - turned)
    filled = (first_holds.astype(F32), second_holds.astype(F32))
    keeps = (1.0 - filled[0] * filled[1], (1.0 - filled[0]) * (1.0 - filled[1]))

    def survey(d, found):
        count = jnp.int32(0)
        for i in range(dp):
            count = count + jnp.where(lax.div(slot_ref[i], jnp.int32(slots)) == d, jnp.int32(1), jnp.int32(0))
        return jnp.where(count == 0, d, found[0]), jnp.where(count > 1, d, found[1])

    lone, crowded = lax.fori_loop(0, dp, survey, (jnp.int32(0), jnp.int32(0)))
    lone_slot = lone * slots + 1
    at_lone = keeps[1]
    inner = 2
    outer = dp // inner
    my_inner = lax.rem(me_d, inner)
    my_outer = lax.div(me_d, inner)

    sends = []

    def send(*args):
        copy = remote(*args)
        copy.start()
        sends.append(copy)

    def start(*args):
        remote(*args).start()

    loads = [
        (vision_h, vis), (kg_h, kgs), (vg_h, vgs),
        (text_h, text), (wk_h, wk), (wv_h, wv), (wp_h, wp),
        (kg4.at[:, me_d], r1k.at[pl.ds(me_d * slots, slots)]),
        (vg4.at[:, me_d], r1v.at[pl.ds(me_d * slots, slots)]),
    ]
    loads = [pltpu.make_async_copy(a, b, load_sem.at[n]) for n, (a, b) in enumerate(loads)]
    for copy in loads:
        copy.start()

    barrier = pltpu.get_barrier_semaphore()

    @pl.loop(1, dp)
    def _(k):
        pl.semaphore_signal(barrier, inc=1, device_id=(dnext(k), me), device_id_type=pl.DeviceIdType.MESH)

    for k in range(1, mp):
        pl.semaphore_signal(
            barrier, inc=1, device_id=(me_d, lax.rem(me + k, mp)), device_id_type=pl.DeviceIdType.MESH
        )

    loads[0].wait()
    vf = vis[...].astype(F32)
    vscale = lax.rsqrt(jnp.mean(vf * vf, axis=1, keepdims=True) + 1e-06)
    vis_gain = gain_row(vgain)
    vis_all[me] = (vf * vscale * vis_gain).astype(BF16)
    pl.semaphore_wait(barrier, dp - 1 + mp - 1)
    mine = pl.ds(me_d * slots, slots)
    others = pl.ds(0, dp - 1)

    def a1(k, which):
        src, dst = ((kg4, r1k), (vg4, r1v))[which]
        return remote(
            src.at[:, dnext(k)], dst.at[mine], a1_s.at[which], a1_r.at[which], (dnext(k), me)
        )

    @pl.loop(1, dp)
    def _(k):
        a1(k, 0).start()
        a1(k, 1).start()


    def gather_start(g, block):
        for k in range(1, ycount):
            send(block(me), block(me), ag_s.at[g, k], ag_r.at[g, k], (me_d, ynext(k) * 2 + core))
        send(block(me), block(me), ag_s.at[g, 0], ag_r.at[g, 0], (me_d, partner))

    def arrived(block, send_sem, recv_sem):
        remote(block, block, send_sem, recv_sem, (me_d, partner)).wait_recv()

    def gather_relay(g, block):
        for k in range(1, ycount):
            got = block(yprev(k) * 2 + core)
            arrived(got, ag_s.at[g, k], ag_r.at[g, k])
            send(got, got, ag_s.at[g, ycount + k - 1], ag_r.at[g, ycount + k - 1], (me_d, partner))

    def gather_finish(g, block):
        arrived(block(partner), ag_s.at[g, 0], ag_r.at[g, 0])
        for k in range(1, ycount):
            arrived(block(yprev(k) * 2 + 1 - core), ag_s.at[g, ycount + k - 1], ag_r.at[g, ycount + k - 1])

    vis_block = lambda m: vis_all.at[m]
    gk_block = lambda m: gk.at[:, col(m)]
    gv_block = lambda m: gv.at[:, col(m)]
    gik_block = lambda m: gik.at[:, col(m)]
    giv_block = lambda m: giv.at[:, col(m)]

    gather_start(0, vis_block)

    loads[1].wait()
    loads[2].wait()
    for p in range(slots):
        gk[p * PATCH:(p + 1) * PATCH, col(me)] = kgs[slot_at[p]]
        gv[p * PATCH:(p + 1) * PATCH, col(me)] = vgs[slot_at[p]]
    first_rows = pl.ds(0, PATCH)
    later_rows = pl.ds(PATCH, PATCH)
    gka_block = lambda m: gk.at[first_rows, col(m)]
    gva_block = lambda m: gv.at[first_rows, col(m)]

    def pair_start(g, block, whole):
        for k in range(1, ycount):
            send(block(me), block(me), ag_s.at[g, k], ag_r.at[g, k], (me_d, ynext(k) * 2 + core))
        send(whole(me), whole(me), ag_s.at[g, 0], ag_r.at[g, 0], (me_d, partner))

    def near_finish(g, block):
        arrived(block(partner), ag_s.at[g, 0], ag_r.at[g, 0])

    def far_finish(g, block):
        for k in range(1, ycount):
            arrived(block(yprev(k) * 2 + 1 - core), ag_s.at[g, ycount + k - 1], ag_r.at[g, ycount + k - 1])

    def heads(yk):
        return pl.ds(pl.multiple_of(yk * 2 * kvd, 2 * kvd), 2 * kvd)

    def products(keys, values, at, cs, yk):
        at_heads = heads(yk)
        return nt(keys[at, at_heads], wk[cs, at_heads]) + nt(values[at, at_heads], wv[cs, at_heads])

    def far_products(keys, values, at, cs):
        total = products(keys, values, at, cs, ynext(1))
        for k in range(2, ycount):
            total = total + products(keys, values, at, cs, ynext(k))
        return total

    step = 256
    every = pl.ds(0, tokens)
    image_rows = pl.ds(0, img_rows)

    pair_start(1, gka_block, gk_block)
    pair_start(2, gva_block, gv_block)

    def chunk(x, m):
        k_part = jnp.dot(x[...], wk[:, col(m)], preferred_element_type=F32)
        v_part = jnp.dot(x[...], wv[:, col(m)], preferred_element_type=F32)
        return k_part, v_part

    def stage_send(x, n, psend, l1):
        for k in range(ycount):
            yk = ynext(k)
            k_part, v_part = chunk(x, yk * 2 + 1 - core)
            shape = psend.shape[1:-1] + (kvd,)
            psend[yk, ..., :kvd] = k_part.astype(BF16).reshape(shape)
            psend[yk, ..., kvd:] = v_part.astype(BF16).reshape(shape)
            start(psend.at[yk], l1.at[yk], rs_s.at[n, 0], rs_r.at[n, k], (me_d, partner))

    def stage_own(x, own):
        for k in range(ycount):
            yk = ynext(k)
            k_part, v_part = chunk(x, yk * 2 + core)
            shape = own.shape[1:-1] + (kvd,)
            own[yk, ..., :kvd] = k_part.reshape(shape)
            own[yk, ..., kvd:] = v_part.reshape(shape)

    def level_two(n, own, l1, s2, l2):
        for k in range(ycount - 1, 0, -1):
            yk = ynext(k)
            arrived(l1.at[yk], rs_s.at[n, 0], rs_r.at[n, k])
            s2[k] = (own[yk] + l1[yk].astype(F32)).astype(BF16)

    def level_go(n, s2, l2):
        for k in range(ycount - 1, 0, -1):
            start(s2.at[k], l2.at[k], rs_s.at[n, k], rs1_r.at[k - 1], (me_d, ynext(k) * 2 + core))

    def level_end(n, own, l1, l2):
        arrived(l1.at[y], rs_s.at[n, 0], rs_r.at[n, 0])
        total = own[y] + l1[y].astype(F32)
        for k in range(1, ycount):
            arrived(l2.at[k], rs_s.at[n, k], rs1_r.at[k - 1])
            total = total + l2[k].astype(F32)
        return total

    def text_piece(p, k):
        at = pl.ds(p * piece_rows, piece_rows)
        return remote(
            t_s2.at[k, at], t_l2.at[k, at], rs_s.at[0, k], t2_r.at[k - 1, p], (me_d, ynext(k) * 2 + core)
        )

    def text_go(p):
        for k in range(ycount - 1, 0, -1):
            text_piece(p, k).start()

    def stats_send(n, st, sr):
        for k in range(1, mp):
            start(st, sr.at[k], st_s.at[n], st_r.at[n], (me_d, lax.rem(me + k, mp)))

    def stats_total(n, st, sr):
        total = st[...]
        arrived(sr.at[pl.ds(1, mp - 1)], st_s.at[n], st_r.at[n])
        for k in range(1, mp):
            total = total + sr[k]
        return to_columns(total)

    def wide(p):
        return jnp.concatenate([p] * (step // 128), axis=1)

    def fold(p):
        total = p[:, :128]
        for n in range(1, p.shape[1] // 128):
            total = total + p[:, n * 128:(n + 1) * 128]
        return total

    loads[3].wait()
    for p in range(slots):
        tf = text[slot_at[p]].astype(F32)
        sc_t[p] = fold(tf * tf)
        xt[p * PATCH:(p + 1) * PATCH, :] = (tf * gain[...]).astype(BF16)
    loads[4].wait()
    loads[5].wait()
    stage_send(xt, 0, t_send, t_l1)
    stage_own(xt, t_own)
    for k in range(ycount - 1, 0, -1):
        yk = ynext(k)
        arrived(t_l1.at[yk], rs_s.at[0, 0], rs_r.at[0, k])
        t_s2[k] = (t_own[yk, 0] + t_l1[yk, 0].astype(F32)).astype(BF16)
        rest = t_own[yk, 1] + t_l1[yk, 1].astype(F32)
        tb_send[:, k - 1] = rest.reshape(dp, rb, 2 * kvd).astype(BF16)
    tb_recv[me_d] = tb_send[me_d]
    near_finish(1, gk_block)
    near_finish(2, gv_block)

    def text_near(j, _):
        cs = pl.ds(pl.multiple_of(j * step, step), step)
        dt[:, :, cs] = products(gk, gv, every, cs, y).reshape(slots, PATCH, step)
        return 0

    lax.fori_loop(0, width // step, text_near, 0)
    co_t[...] = jnp.zeros(co_t.shape, F32)
    gather_relay(0, vis_block)
    loads[7].wait()
    loads[8].wait()

    for which, dst in ((0, r1k), (1, r1v)):
        arrived(dst.at[pl.ds(0, (dp - 1) * slots)], a1_s.at[which], a1_r.at[which])

    @pl.loop(0, dp)
    def _(i):
        s2k[i] = r1k[slot_ref[i]]
        s2v[i] = r1v[slot_ref[i]]

    r2k[me_d] = s2k[me_d]
    r2v[me_d] = s2v[me_d]

    def a2(k, which):
        src, dst = ((s2k, r2k), (s2v, r2v))[which]
        return remote(
            src.at[dnext(k)], dst.at[me_d], a2_s.at[which], a2_r.at[which], (dnext(k), me)
        )

    @pl.loop(1, dp)
    def _(k):
        a2(k, 0).start()
        a2(k, 1).start()

    kb_send[0] = r1k[lone_slot]
    kb_send[1] = r1v[lone_slot]
    for k in range(1, ycount):
        send(kb_send, kb_y.at[k - 1], kby_s.at[k - 1], kby_r.at[k - 1], (me_d, ynext(k) * 2 + core))
    text_go(0)
    gather_finish(0, vis_block)
    loads[6].wait()

    sc_i[...] = jnp.zeros(sc_i.shape, F32)

    def project(j, _):
        cs = pl.ds(pl.multiple_of(j * step, step), step)
        e = jnp.concatenate([vis_all[m] for m in range(mp)], axis=0)
        e = jnp.dot(e, wp[:, cs], preferred_element_type=F32).astype(BF16)
        emb[:, cs] = e
        ef = e.astype(F32)
        xi[:, cs] = (ef * gain[:, cs]).astype(BF16)
        sc_i[...] += fold(ef * ef)
        return 0

    lax.fori_loop(0, width // step, project, 0)
    for k in range(1, ycount):
        arrived(kb_y.at[k - 1], kby_s.at[k - 1], kby_r.at[k - 1])
    kbr[me_d] = kb_y[...]

    def kbz(k):
        return remote(kb_y, kbr.at[me_d], kbz_s.at[0], kbz_r.at[0], (dnext(k), me))

    def tbz(k):
        return remote(tb_send.at[dnext(k)], tb_recv.at[me_d], tbz_s.at[0], tbz_r.at[0], (dnext(k), me))

    @pl.loop(1, dp)
    def _(k):
        kbz(k).start()

    @pl.loop(1, dp)
    def _(k):
        tbz(k).start()

    gather_relay(1, gka_block)
    gather_relay(2, gva_block)
    zero = jnp.zeros((img_rows, 1), F32)
    st_q[...] = to_rows(jnp.sum(sc_i[...], axis=1, keepdims=True), zero)
    stats_send(2, st_q, sr_q)

    for which, dst in ((0, r2k), (1, r2v)):
        arrived(dst.at[others], a2_s.at[which], a2_r.at[which])

    own_k = r2k[...].astype(F32).reshape(PATCH, kvd)
    own_v = r2v[...].astype(F32).reshape(PATCH, kvd)
    gik[:, col(me)] = own_k.astype(BF16)
    giv[:, col(me)] = own_v.astype(BF16)
    gather_start(3, gik_block)
    gather_start(4, giv_block)
    stage_send(xi, 1, i_send, i_l1)
    stage_own(xi, i_own)
    level_two(1, i_own, i_l1, i_s2, i_l2)
    level_go(1, i_s2, i_l2)
    far_finish(1, gka_block)
    far_finish(2, gva_block)

    def text_far(p):
        rows_p = pl.ds(p * PATCH, PATCH)

        def body(j, _):
            cs = pl.ds(pl.multiple_of(j * step, step), step)
            d = (dt[p, :, cs] + far_products(gk, gv, rows_p, cs)) * gain[:, cs]
            dt[p, :, cs] = d
            co_t[p] += fold(d * text[slot_at[p], :, cs].astype(F32))
            return 0

        lax.fori_loop(0, width // step, body, 0)

    text_far(0)
    near_finish(3, gik_block)
    near_finish(4, giv_block)

    def image_near(j, _):
        cs = pl.ds(pl.multiple_of(j * step, step), step)
        dg[:, cs] = products(gik, giv, image_rows, cs, y)
        return 0

    lax.fori_loop(0, width // step // 2, image_near, 0)
    gather_relay(3, gik_block)
    gather_relay(4, giv_block)
    lax.fori_loop(width // step // 2, width // step, image_near, 0)
    co_i[...] = jnp.zeros(co_i.shape, F32)

    arrived(kbr.at[others], kbz_s.at[0], kbz_r.at[0])

    for k in range(1, ycount):
        m = yprev(k) * 2 + core
        for which, g in ((0, gk), (1, gv)):
            g[later_rows, col(m)] = kbr[:, k - 1, which].astype(F32).reshape(PATCH, kvd).astype(BF16)
            send(
                g.at[later_rows, col(m)], g.at[later_rows, col(m)], kbp_s.at[which, k - 1], kbp_r.at[which, k - 1],
                (me_d, partner),
            )
    far_finish(3, gik_block)
    far_finish(4, giv_block)

    def image_far(j, _):
        cs = pl.ds(pl.multiple_of(j * step, step), step)
        d = (dg[:, cs] + far_products(gik, giv, image_rows, cs)) * gain[:, cs]
        dg[:, cs] = d
        co_i[...] += fold(d * emb[:, cs].astype(F32))
        return 0

    lax.fori_loop(0, width // step, image_far, 0)
    st_i[...] = to_rows(zero, jnp.sum(co_i[...], axis=1, keepdims=True))
    stats_send(1, st_i, sr_i)
    text_go(1)
    sq_i, _ = stats_total(2, st_q, sr_q)
    scale_i = lax.rsqrt(sq_i / d_model + 1e-05)
    sc_i[...] = jnp.broadcast_to(scale_i, sc_i.shape)
    total = level_end(1, i_own, i_l1, i_l2)
    kvb[...] = (total * sc_i[:, 0:1]).reshape(dp, rb, 2 * kvd).astype(BF16)
    r3[me_d] = kvb[me_d]

    def b1(k):
        return remote(kvb.at[dnext(k)], r3.at[me_d], b1_s.at[0], b1_r.at[0], (dnext(k), me))

    @pl.loop(1, dp)
    def _(k):
        b1(k).start()

    for k in range(1, ycount):
        for which, g in ((0, gk), (1, gv)):
            arrived(g.at[later_rows, col(yprev(k) * 2 + 1 - core)], kbp_s.at[which, k - 1], kbp_r.at[which, k - 1])
    text_far(1)
    st_t[...] = to_rows(
        jnp.sum(sc_t[...].reshape(tokens, 128), axis=1, keepdims=True),
        jnp.sum(co_t[...].reshape(tokens, 128), axis=1, keepdims=True),
    )
    stats_send(0, st_t, sr_t)

    arrived(tb_recv.at[others], tbz_s.at[0], tbz_r.at[0])

    tb_sel[...] = tb_recv[lone]
    for k in range(1, ycount):
        send(tb_sel.at[k - 1], tb_y.at[k - 1], tby_s.at[k - 1], tby_r.at[k - 1], (me_d, ynext(k) * 2 + core))
    _, inner_i = stats_total(1, st_i, sr_i)
    scale_i = sc_i[:, 0:1]
    co_i[...] = jnp.broadcast_to(scale_i * scale_i * scale_i * (inner_i / d_model), co_i.shape)

    def image_end(j, _):
        cs = pl.ds(pl.multiple_of(j * step, step), step)
        d = wide(sc_i[...]) * dg[:, cs] - emb[:, cs].astype(F32) * wide(co_i[...])
        dimg[:, cs] = d.astype(BF16)
        return 0

    lax.fori_loop(0, width // step, image_end, 0)
    cuts = vis_cuts(dv)
    pieces = len(cuts) - 1

    def vis_chunk(j):
        at = pl.ds(cuts[j], cuts[j + 1] - cuts[j])
        d = nt(dimg[...], wp[at, :]).reshape(ycount, 2, rows, cuts[j + 1] - cuts[j])
        for yi in range(ycount):
            a, b = d[yi, 0], d[yi, 1]
            first = core == 0
            d_own[yi, :, at] = jnp.where(first, a, b)
            d_send[yi, :, at] = jnp.where(first, b, a).astype(BF16)
        start(d_send.at[:, :, at], d_l1.at[:, :, at], dv_s.at[0], dv_r.at[j, 0], (me_d, partner))

    def vis_two(j):
        at = pl.ds(cuts[j], cuts[j + 1] - cuts[j])
        arrived(d_l1.at[:, :, at], dv_s.at[0], dv_r.at[j, 0])
        for k in range(1, ycount):
            yk = ynext(k)
            d_s2[k, :, at] = (d_own[yk, :, at] + d_l1[yk, :, at].astype(F32)).astype(BF16)
            start(d_s2.at[k, :, at], d_l2.at[k, :, at], dv_s.at[k], dv_r.at[j, k], (me_d, yk * 2 + core))

    def b2(k):
        return remote(s4.at[dnext(k)], r4.at[0, my_inner, my_outer], b2_s.at[0], b2_r.at[0], (dnext(k), me))

    def b3(k):
        target = lax.rem(my_outer + k, outer) * inner + my_inner
        return remote(s5, r4.at[1, my_inner, my_outer], b3_s.at[0], b3_r.at[0], (target, me))

    def b4():
        block = r4.at[1, my_inner]
        return remote(block, block, b3_s.at[1], b3_r.at[1], (my_outer * inner + 1 - my_inner, me))

    for j in range(pieces):
        vis_chunk(j)
        if j > 0:
            vis_two(j - 1)
        if j == min(2, pieces - 1):

            arrived(r3.at[others], b1_s.at[0], b1_r.at[0])

            extra = jnp.zeros((rb, 2 * kvd), F32)
            for k in range(1, ycount):
                arrived(tb_y.at[k - 1], tby_s.at[k - 1], tby_r.at[k - 1])
                extra = extra + tb_y[k - 1].astype(F32)
            r3[dp] = extra.astype(BF16)

            @pl.loop(0, dp)
            def _(d):
                source = owner_of(d * slots + 1)
                source = jnp.where(is_filled(d * slots) == 1, owner_of(d * slots), source)
                s4[d] = r3[jnp.where(d == lone, jnp.int32(dp), source)]

            s5[...] = r3[owner_of(crowded * slots + 1)]
            r4[0, my_inner, my_outer] = s4[me_d]
            r4[1, my_inner, my_outer] = s5[...]

            @pl.loop(1, outer)
            def _(k):
                b3(k).start()

            @pl.loop(1, dp)
            def _(k):
                b2(k).start()

    vis_two(pieces - 1)
    arrived(r4.at[1, my_inner, pl.ds(0, outer - 1)], b3_s.at[0], b3_r.at[0])
    b4().start()
    sq_t, inner_t = stats_total(0, st_t, sr_t)
    keep = jnp.concatenate([jnp.full((PATCH, 1), 1.0, F32) * keeps[p] for p in range(slots)], axis=0)
    scale_t = lax.rsqrt(sq_t / d_model + 1e-05)
    sc_t[...] = jnp.broadcast_to(scale_t * keep, (tokens, 128)).reshape(sc_t.shape)
    co_t[...] = jnp.broadcast_to(
        scale_t * scale_t * scale_t * (inner_t / d_model) * keep, (tokens, 128)
    ).reshape(co_t.shape)

    def text_back(j, _):
        cs = pl.ds(pl.multiple_of(j * step, step), step)
        for s in range(slots):
            at = place_of[s]
            d = wide(sc_t[at]) * dt[at, :, cs] - text[s, :, cs].astype(F32) * wide(co_t[at])
            tg[s * PATCH:(s + 1) * PATCH, cs] = d.astype(BF16)
        return 0

    lax.fori_loop(0, width // step, text_back, 0)
    vf = vis[...].astype(F32)
    vscale = lax.rsqrt(jnp.mean(vf * vf, axis=1, keepdims=True) + 1e-06)
    hs = []
    for j in range(pieces):
        at = pl.ds(cuts[j], cuts[j + 1] - cuts[j])
        d = d_own[y, :, at] + d_l1[y, :, at].astype(F32)
        for k in range(1, ycount):
            arrived(d_l2.at[k, :, at], dv_s.at[k], dv_r.at[j, k])
            d = d + d_l2[k, :, at].astype(F32)
        hs.append(d.astype(BF16).astype(F32))
    h = jnp.concatenate(hs, axis=1) * gain_row(vgain)
    v_inner = jnp.mean(h * vf, axis=1, keepdims=True)
    vg_out[...] = (vscale * h - vf * vscale * vscale * vscale * v_inner).astype(BF16)

    arrived(s4.at[others], b2_s.at[0], b2_r.at[0])
    arrived(r4.at[1, 1 - my_inner], b3_s.at[1], b3_r.at[1])

    arrived(t_l1.at[y], rs_s.at[0, 0], rs_r.at[0, 0])
    for p in range(t_pieces):
        for k in range(1, ycount):
            text_piece(p, k).wait_recv()
    direct = t_l2[1].astype(F32)
    for k in range(2, ycount):
        direct = direct + t_l2[k].astype(F32)
    for s in range(slots):
        at = place_of[s]
        is_first = 1.0 - at.astype(F32)
        which = s * first_holds * second_holds
        placed = jnp.concatenate([r4[which, r % inner, r // inner] for r in range(dp)], axis=0).astype(F32)
        total = t_own[y, at] + t_l1[y, at].astype(F32) + direct * is_first + placed * ((1.0 - is_first) * at_lone)
        out = total * sc_t[at][:, 0:1] + placed * filled[s]
        rows_s = pl.ds(s * PATCH, PATCH)
        k_out[rows_s, :] = out[:, :kvd].astype(BF16)
        v_out[rows_s, :] = out[:, kvd:].astype(BF16)
    for copy in sends:
        copy.wait_send()

    def sent(block, sem):
        remote(block, block, sem, ag_r.at[0, 0], (me_d, partner)).wait_send()

    for which, (first, second) in enumerate(((kg4, s2k), (vg4, s2v))):
        sent(first.at[:, others], a1_s.at[which])
        sent(second.at[others], a2_s.at[which])
    sent(kvb.at[others], b1_s.at[0])
    sent(s4.at[others], b2_s.at[0])
    sent(r4.at[1, my_inner, pl.ds(0, outer - 1)], b3_s.at[0])
    sent(r4.at[1, my_inner], b3_s.at[1])
    sent(kbr.at[others], kbz_s.at[0])
    sent(tb_send.at[others], tbz_s.at[0])
    sent(t_send, rs_s.at[0, 0])
    sent(i_send, rs_s.at[1, 0])
    sent(d_send, dv_s.at[0])
    for k in range(1, ycount):
        sent(t_s2.at[k], rs_s.at[0, k])
        sent(i_s2.at[k], rs_s.at[1, k])
        sent(d_s2.at[k], dv_s.at[k])
    for n, sr in enumerate((sr_t, sr_i, sr_q)):
        sent(sr.at[pl.ds(0, mp - 1)], st_s.at[n])


def shards(vision, vision_gain, image_slot, text_embed, w_proj, llm_gain, w_key, w_value, key_grad, value_grad):
    dp = lax.axis_size("dp")
    mp = lax.axis_size("mp")
    tokens, width = text_embed.shape
    slots = tokens // PATCH
    rows, dv = vision.shape
    kvd = key_grad.shape[1]
    kv = kvd * mp
    img = rows * mp
    rb = PATCH // dp
    ys = mp // 2
    pieces = len(vis_cuts(dv)) - 1
    V = pltpu.VMEM
    any_spec = pl.BlockSpec(memory_space=pl.ANY)
    vmem = pl.BlockSpec(memory_space=pltpu.VMEM)
    smem = pl.BlockSpec(memory_space=pltpu.SMEM)
    scratch = [
        V((rows, dv), BF16), V((mp, rows, dv), BF16), V((slots, PATCH, width), BF16), V((dv, width), BF16),
        V((width, kv), BF16), V((width, kv), BF16), V((tokens, width), BF16),
        V((tokens, kv), BF16), V((tokens, kv), BF16), V((img, kv), BF16), V((img, kv), BF16),
        V((img, width), BF16), V((img, width), BF16), V((img, width), BF16), V((img, width), F32),
    ]
    t_shape = (ys, slots, PATCH, 2 * kvd)
    i_shape = (ys, img, 2 * kvd)
    half = (ys, PATCH, 2 * kvd)
    scratch += [V(t_shape, BF16), V(t_shape, F32), V(t_shape, BF16), V(half, BF16), V(half, BF16)]
    scratch += [V(i_shape, BF16), V(i_shape, F32), V(i_shape, BF16), V(i_shape, BF16), V(i_shape, BF16)]
    scratch += [
        V((ys, rows, dv), BF16), V((ys, rows, dv), F32), V((ys, rows, dv), BF16), V((ys, rows, dv), BF16),
        V((ys, rows, dv), BF16),
        V((8, tokens), F32), V((mp, 8, tokens), F32), V((8, img), F32), V((mp, 8, img), F32),
        V((8, img), F32), V((mp, 8, img), F32),
        V((slots, PATCH, 128), F32), V((slots, PATCH, 128), F32), V((img, 128), F32), V((img, 128), F32),
        V((slots, PATCH, kvd), BF16), V((slots, PATCH, kvd), BF16),
        V((2, rb, kvd), BF16), V((ys - 1, 2, rb, kvd), BF16), V((dp, ys - 1, 2, rb, kvd), BF16),
        V((dp, ys - 1, rb, 2 * kvd), BF16), V((dp, ys - 1, rb, 2 * kvd), BF16),
        V((ys - 1, rb, 2 * kvd), BF16), V((ys - 1, rb, 2 * kvd), BF16),
        V((dp * slots, rb, kvd), BF16), V((dp * slots, rb, kvd), BF16),
        V((dp, rb, kvd), BF16), V((dp, rb, kvd), BF16), V((dp, rb, kvd), BF16), V((dp, rb, kvd), BF16),
        V((dp, rb, 2 * kvd), BF16), V((dp + 1, rb, 2 * kvd), BF16),
        V((dp, rb, 2 * kvd), BF16), V((rb, 2 * kvd), BF16), V((2, 2, dp // 2, rb, 2 * kvd), BF16),
        DMA((9,)), DMA((5, 2 * ys - 1)), DMA((5, 2 * ys - 1)), DMA((2, ys)), DMA((2, ys)), DMA((ys - 1,)),
        DMA((ys - 1, 2)), DMA((3,)), DMA((3,)), DMA((ys,)), DMA((pieces, ys)),
        DMA((2,)), DMA((2,)), DMA((2,)), DMA((2,)),
        DMA((1,)), DMA((1,)), DMA((1,)), DMA((1,)), DMA((2,)), DMA((2,)),
        DMA((ys - 1,)), DMA((ys - 1,)), DMA((1,)), DMA((1,)), DMA((2, ys - 1)), DMA((2, ys - 1)),
        DMA((1,)), DMA((1,)), DMA((ys - 1,)), DMA((ys - 1,)), V((slots, PATCH, width), F32),
    ]
    shapes = ((tokens, kvd), (tokens, kvd), (tokens, width), (rows, dv))
    room = sum(2 * a * b for a, b in shapes)
    lanes = 128 if dv % 128 == 0 else dv
    results = pl.pallas_call(
        functools.partial(kernel, dp, mp),
        out_shape=tuple(V(shape, BF16) for shape in shapes),
        in_specs=[smem, any_spec, vmem, any_spec, any_spec, vmem] + [any_spec] * 6,
        out_specs=(vmem,) * len(shapes),
        scratch_shapes=scratch,
        compiler_params=pltpu.CompilerParams(
            collective_id=0, has_side_effects=True, vmem_limit_bytes=67043328 - room
        ),
    )(
        image_slot, vision, vision_gain.reshape(-1, lanes), text_embed.reshape(slots, PATCH, width), w_proj,
        llm_gain[None, :], w_key, w_value, key_grad.reshape(slots, PATCH, kvd), value_grad.reshape(slots, PATCH, kvd),
        key_grad.reshape(slots, dp, rb, kvd), value_grad.reshape(slots, dp, rb, kvd),
    )
    return pl.pallas_call(
        write_out,
        out_shape=tuple(jax.ShapeDtypeStruct(shape, BF16) for shape in shapes),
        in_specs=[vmem] * len(shapes),
        out_specs=(any_spec,) * len(shapes),
        scratch_shapes=[DMA((len(shapes),))],
        compiler_params=pltpu.CompilerParams(vmem_limit_bytes=1 << 20),
    )(*results)


def solution(mesh):
    placed = (
        P(("dp", "mp"), None),
        P(),
        P(),
        P("dp", "mp"),
        P(None, "mp"),
        P("mp"),
        P("mp", None),
        P("mp", None),
        P("dp", "mp"),
        P("dp", "mp"),
    )
    return jax.shard_map(
        shards,
        mesh=mesh,
        in_specs=placed,
        out_specs=(P("dp", "mp"), P("dp", "mp"), P("dp", "mp"), P(("dp", "mp"), None)),
        check_vma=False,
    )
```

time: 67.3 us -> 61.1 us (0.908)
  the two profiles are of different devices: /device:TPU:11 before, /device:TPU:0 now
where the time goes in v4:
time: 61.1 us; the launch traced here: 60.9 us
  Pallas kernels  60.1 us (98%)
  between operations  0.8 us (1%)
    pallas_call x1, Pallas kernels, shards(): pl.pallas_call(functools.partial(kernel, dp, mp), out_shape=tuple((V(shap...  58.4 us
    pallas_call x1, Pallas kernels, shards(): pl.pallas_call(write_out, out_shape=tuple((jax.ShapeDtypeStruct(shape, BF...  1.65 us

profile of v4, /device:TPU:0, one launch (start us, length us, event | category | flops | bytes accessed | tf_op | source)
XLA Modules:
  0.0 60.9 jit_solution(5799883129691112208)
XLA Ops:
  0.6 58.4 %shard_map.129 = (bf16[512,256]{1,0:T(8,128)(2,1)S(1)}, bf16[512,256]{1,0:T(8,128)(2,1)S(1)}, bf16[512,2048]{1,0:T(8,128)(2,1)S(1)}, bf16[64,3200]{1,0:T(8,128)(2,1)S(1)}) custom-call(s32[8]{0:T(128)} %slot_ref.1, bf16[64,3200]{1,0:T(8,128)(2,1)} %vision_h.1, f32[25,128]{1,0:T(8,128)} %bitcast.12, bf16[2,256,2048]{2,1,0:T(8,128)(2,1)} %bitcast.7, ...), custom_call_target="tpu_custom_call" | custom-call | tf_op jit(solution)/shard_map/pallas_call | solution.py:736
  59.1 1.7 %shard_map.130 = (bf16[512,256]{1,0:T(8,128)(2,1)}, bf16[512,256]{1,0:T(8,128)(2,1)}, bf16[512,2048]{1,0:T(8,128)(2,1)}, bf16[64,3200]{1,0:T(8,128)(2,1)}) custom-call(bf16[512,256]{1,0:T(8,128)(2,1)S(1)} %get-tuple-element.8.refs_0_, bf16[512,256]{1,0:T(8,128)(2,1)S(1)} %get-tuple-element.9.refs_1_, bf16[512,2048]{1,0:T(8,128)(2,1)S(1)} %get-tuple-element.10.refs_2_, ...), custom_call_target="tpu_custom_call" | custom-call | tf_op jit(solution)/shard_map/pallas_call | solution.py:750

commit v5 on v4

--- a/solution.py
+++ b/solution.py
@@ -47,9 +47,11 @@
         return (0, dv)
     units = dv // 128
     first = max(units // 12, 1)
-    cuts = [0, first]
+    cuts = [0, first, min(2 * first, units)]
     while cuts[-1] < units:
-        cuts.append(min(cuts[-1] + max(units // 5, 1), units))
+        cuts.append(min(cuts[-1] + 2 * first, units))
+    if len(cuts) > 3 and cuts[-1] - cuts[-2] < first:
+        del cuts[-2]
     return tuple(128 * c for c in cuts)
 
 
@@ -122,26 +124,21 @@
     def holds(s):
         return is_filled(me_d * slots + s)
 
-    first_holds, second_holds = holds(0), holds(1)
-    turned = first_holds * (1 - second_holds)
-    slot_at = (turned, 1 - turned)
-    place_of = (turned, 1 - turned)
-    filled = (first_holds.astype(F32), second_holds.astype(F32))
-    keeps = (1.0 - filled[0] * filled[1], (1.0 - filled[0]) * (1.0 - filled[1]))
-
-    def survey(d, found):
-        count = jnp.int32(0)
-        for i in range(dp):
-            count = count + jnp.where(lax.div(slot_ref[i], jnp.int32(slots)) == d, jnp.int32(1), jnp.int32(0))
-        return jnp.where(count == 0, d, found[0]), jnp.where(count > 1, d, found[1])
-
-    lone, crowded = lax.fori_loop(0, dp, survey, (jnp.int32(0), jnp.int32(0)))
-    lone_slot = lone * slots + 1
-    at_lone = keeps[1]
     inner = 2
     outer = dp // inner
     my_inner = lax.rem(me_d, inner)
     my_outer = lax.div(me_d, inner)
+
+    barrier = pltpu.get_barrier_semaphore()
+
+    @pl.loop(1, dp)
+    def _(k):
+        pl.semaphore_signal(barrier, inc=1, device_id=(dnext(k), me), device_id_type=pl.DeviceIdType.MESH)
+
+    for k in range(1, mp):
+        pl.semaphore_signal(
+            barrier, inc=1, device_id=(me_d, lax.rem(me + k, mp)), device_id_type=pl.DeviceIdType.MESH
+        )
 
     sends = []
 
@@ -163,64 +160,60 @@
     for copy in loads:
         copy.start()
 
-    barrier = pltpu.get_barrier_semaphore()
+    pl.semaphore_wait(barrier, dp - 1 + mp - 1)
+    mine = pl.ds(me_d * slots, slots)
+    others = pl.ds(0, dp - 1)
+
+    def a1(k, which):
+        src, dst = ((kg4, r1k), (vg4, r1v))[which]
+        return remote(
+            src.at[:, dnext(k)], dst.at[mine], a1_s.at[which], a1_r.at[which], (dnext(k), me)
+        )
 
     @pl.loop(1, dp)
     def _(k):
-        pl.semaphore_signal(barrier, inc=1, device_id=(dnext(k), me), device_id_type=pl.DeviceIdType.MESH)
-
-    for k in range(1, mp):
-        pl.semaphore_signal(
-            barrier, inc=1, device_id=(me_d, lax.rem(me + k, mp)), device_id_type=pl.DeviceIdType.MESH
-        )
+        a1(k, 0).start()
+        a1(k, 1).start()
+
+
+    def gather_start(g, block):
+        for k in range(1, ycount):
+            send(block(me), block(me), ag_s.at[g, k], ag_r.at[g, k], (me_d, ynext(k) * 2 + core))
+        send(block(me), block(me), ag_s.at[g, 0], ag_r.at[g, 0], (me_d, partner))
+
+    def arrived(block, send_sem, recv_sem):
+        remote(block, block, send_sem, recv_sem, (me_d, partner)).wait_recv()
+
+    def gather_relay(g, block):
+        for k in range(1, ycount):
+            got = block(yprev(k) * 2 + core)
+            arrived(got, ag_s.at[g, k], ag_r.at[g, k])
+            send(got, got, ag_s.at[g, ycount + k - 1], ag_r.at[g, ycount + k - 1], (me_d, partner))
+
+    def gather_finish(g, block):
+        arrived(block(partner), ag_s.at[g, 0], ag_r.at[g, 0])
+        for k in range(1, ycount):
+            arrived(block(yprev(k) * 2 + 1 - core), ag_s.at[g, ycount + k - 1], ag_r.at[g, ycount + k - 1])
+
+    vis_block = lambda m: vis_all.at[m]
+    gk_block = lambda m: gk.at[:, col(m)]
+    gv_block = lambda m: gv.at[:, col(m)]
+    gik_block = lambda m: gik.at[:, col(m)]
+    giv_block = lambda m: giv.at[:, col(m)]
 
     loads[0].wait()
     vf = vis[...].astype(F32)
     vscale = lax.rsqrt(jnp.mean(vf * vf, axis=1, keepdims=True) + 1e-06)
     vis_gain = gain_row(vgain)
     vis_all[me] = (vf * vscale * vis_gain).astype(BF16)
-    pl.semaphore_wait(barrier, dp - 1 + mp - 1)
-    mine = pl.ds(me_d * slots, slots)
-    others = pl.ds(0, dp - 1)
-
-    def a1(k, which):
-        src, dst = ((kg4, r1k), (vg4, r1v))[which]
-        return remote(
-            src.at[:, dnext(k)], dst.at[mine], a1_s.at[which], a1_r.at[which], (dnext(k), me)
-        )
-
-    @pl.loop(1, dp)
-    def _(k):
-        a1(k, 0).start()
-        a1(k, 1).start()
-
-
-    def gather_start(g, block):
-        for k in range(1, ycount):
-            send(block(me), block(me), ag_s.at[g, k], ag_r.at[g, k], (me_d, ynext(k) * 2 + core))
-        send(block(me), block(me), ag_s.at[g, 0], ag_r.at[g, 0], (me_d, partner))
-
-    def arrived(block, send_sem, recv_sem):
-        remote(block, block, send_sem, recv_sem, (me_d, partner)).wait_recv()
-
-    def gather_relay(g, block):
-        for k in range(1, ycount):
-            got = block(yprev(k) * 2 + core)
-            arrived(got, ag_s.at[g, k], ag_r.at[g, k])
-            send(got, got, ag_s.at[g, ycount + k - 1], ag_r.at[g, ycount + k - 1], (me_d, partner))
-
-    def gather_finish(g, block):
-        arrived(block(partner), ag_s.at[g, 0], ag_r.at[g, 0])
-        for k in range(1, ycount):
-            arrived(block(yprev(k) * 2 + 1 - core), ag_s.at[g, ycount + k - 1], ag_r.at[g, ycount + k - 1])
-
-    vis_block = lambda m: vis_all.at[m]
-    gk_block = lambda m: gk.at[:, col(m)]
-    gv_block = lambda m: gv.at[:, col(m)]
-    gik_block = lambda m: gik.at[:, col(m)]
-    giv_block = lambda m: giv.at[:, col(m)]
-
     gather_start(0, vis_block)
+
+    first_holds, second_holds = holds(0), holds(1)
+    turned = first_holds * (1 - second_holds)
+    slot_at = (turned, 1 - turned)
+    place_of = (turned, 1 - turned)
+    filled = (first_holds.astype(F32), second_holds.astype(F32))
+    keeps = (1.0 - filled[0] * filled[1], (1.0 - filled[0]) * (1.0 - filled[1]))
 
     loads[1].wait()
     loads[2].wait()
@@ -232,10 +225,12 @@
     gka_block = lambda m: gk.at[first_rows, col(m)]
     gva_block = lambda m: gv.at[first_rows, col(m)]
 
-    def pair_start(g, block, whole):
+    def far_start(g, block):
         for k in range(1, ycount):
             send(block(me), block(me), ag_s.at[g, k], ag_r.at[g, k], (me_d, ynext(k) * 2 + core))
-        send(whole(me), whole(me), ag_s.at[g, 0], ag_r.at[g, 0], (me_d, partner))
+
+    def near_start(g, block):
+        send(block(me), block(me), ag_s.at[g, 0], ag_r.at[g, 0], (me_d, partner))
 
     def near_finish(g, block):
         arrived(block(partner), ag_s.at[g, 0], ag_r.at[g, 0])
@@ -251,18 +246,25 @@
         at_heads = heads(yk)
         return nt(keys[at, at_heads], wk[cs, at_heads]) + nt(values[at, at_heads], wv[cs, at_heads])
 
+    def turned_products(keys, values, at, cs, yk):
+        at_heads = heads(yk)
+        return nt(wk[cs, at_heads], keys[at, at_heads]) + nt(wv[cs, at_heads], values[at, at_heads])
+
     def far_products(keys, values, at, cs):
-        total = products(keys, values, at, cs, ynext(1))
+        total = turned_products(keys, values, at, cs, ynext(1))
         for k in range(2, ycount):
-            total = total + products(keys, values, at, cs, ynext(k))
-        return total
+            total = total + turned_products(keys, values, at, cs, ynext(k))
+        return jnp.transpose(total)
 
     step = 256
+    big = min(1024, width)
     every = pl.ds(0, tokens)
     image_rows = pl.ds(0, img_rows)
 
-    pair_start(1, gka_block, gk_block)
-    pair_start(2, gva_block, gv_block)
+    far_start(1, gka_block)
+    far_start(2, gva_block)
+    near_start(1, gk_block)
+    near_start(2, gv_block)
 
     def chunk(x, m):
         k_part = jnp.dot(x[...], wk[:, col(m)], preferred_element_type=F32)
@@ -294,15 +296,12 @@
 
     def level_go(n, s2, l2):
         for k in range(ycount - 1, 0, -1):
-            start(s2.at[k], l2.at[k], rs_s.at[n, k], rs1_r.at[k - 1], (me_d, ynext(k) * 2 + core))
-
-    def level_end(n, own, l1, l2):
-        arrived(l1.at[y], rs_s.at[n, 0], rs_r.at[n, 0])
-        total = own[y] + l1[y].astype(F32)
-        for k in range(1, ycount):
-            arrived(l2.at[k], rs_s.at[n, k], rs1_r.at[k - 1])
-            total = total + l2[k].astype(F32)
-        return total
+            for h in range(2):
+                at = pl.ds(h * kvd, kvd)
+                start(
+                    s2.at[k, :, at], l2.at[k, :, at], rs_s.at[n, k], rs1_r.at[k - 1, h],
+                    (me_d, ynext(k) * 2 + core),
+                )
 
     def text_piece(p, k):
         at = pl.ds(p * piece_rows, piece_rows)
@@ -358,9 +357,19 @@
         dt[:, :, cs] = products(gk, gv, every, cs, y).reshape(slots, PATCH, step)
         return 0
 
-    lax.fori_loop(0, width // step, text_near, 0)
+    lax.fori_loop(0, width // step // 2, text_near, 0)
+    lax.fori_loop(width // step // 2, width // step, text_near, 0)
     co_t[...] = jnp.zeros(co_t.shape, F32)
     gather_relay(0, vis_block)
+    def survey(d, found):
+        count = jnp.int32(0)
+        for i in range(dp):
+            count = count + jnp.where(lax.div(slot_ref[i], jnp.int32(slots)) == d, jnp.int32(1), jnp.int32(0))
+        return jnp.where(count == 0, d, found[0]), jnp.where(count > 1, d, found[1])
+
+    lone, crowded = lax.fori_loop(0, dp, survey, (jnp.int32(0), jnp.int32(0)))
+    lone_slot = lone * slots + 1
+    at_lone = keeps[1]
     loads[7].wait()
     loads[8].wait()
 
@@ -451,27 +460,26 @@
         rows_p = pl.ds(p * PATCH, PATCH)
 
         def body(j, _):
-            cs = pl.ds(pl.multiple_of(j * step, step), step)
+            cs = pl.ds(pl.multiple_of(j * big, big), big)
             d = (dt[p, :, cs] + far_products(gk, gv, rows_p, cs)) * gain[:, cs]
             dt[p, :, cs] = d
             co_t[p] += fold(d * text[slot_at[p], :, cs].astype(F32))
             return 0
 
-        lax.fori_loop(0, width // step, body, 0)
+        lax.fori_loop(0, width // big, body, 0)
 
     text_far(0)
     near_finish(3, gik_block)
     near_finish(4, giv_block)
 
     def image_near(j, _):
-        cs = pl.ds(pl.multiple_of(j * step, step), step)
-        dg[:, cs] = products(gik, giv, image_rows, cs, y)
+        cs = pl.ds(pl.multiple_of(j * big, big), big)
+        dg[:, cs] = jnp.transpose(turned_products(gik, giv, image_rows, cs, y))
         return 0
 
-    lax.fori_loop(0, width // step // 2, image_near, 0)
+    lax.fori_loop(0, width // big, image_near, 0)
     gather_relay(3, gik_block)
     gather_relay(4, giv_block)
-    lax.fori_loop(width // step // 2, width // step, image_near, 0)
     co_i[...] = jnp.zeros(co_i.shape, F32)
 
     arrived(kbr.at[others], kbz_s.at[0], kbz_r.at[0])
@@ -488,34 +496,43 @@
     far_finish(4, giv_block)
 
     def image_far(j, _):
-        cs = pl.ds(pl.multiple_of(j * step, step), step)
+        cs = pl.ds(pl.multiple_of(j * big, big), big)
         d = (dg[:, cs] + far_products(gik, giv, image_rows, cs)) * gain[:, cs]
         dg[:, cs] = d
         co_i[...] += fold(d * emb[:, cs].astype(F32))
         return 0
 
-    lax.fori_loop(0, width // step, image_far, 0)
+    lax.fori_loop(0, width // big, image_far, 0)
     st_i[...] = to_rows(zero, jnp.sum(co_i[...], axis=1, keepdims=True))
     stats_send(1, st_i, sr_i)
     text_go(1)
     sq_i, _ = stats_total(2, st_q, sr_q)
     scale_i = lax.rsqrt(sq_i / d_model + 1e-05)
     sc_i[...] = jnp.broadcast_to(scale_i, sc_i.shape)
-    total = level_end(1, i_own, i_l1, i_l2)
-    kvb[...] = (total * sc_i[:, 0:1]).reshape(dp, rb, 2 * kvd).astype(BF16)
-    r3[me_d] = kvb[me_d]
-
-    def b1(k):
-        return remote(kvb.at[dnext(k)], r3.at[me_d], b1_s.at[0], b1_r.at[0], (dnext(k), me))
-
-    @pl.loop(1, dp)
-    def _(k):
-        b1(k).start()
-
+
+    def b1(k, h):
+        return remote(kvb.at[h, dnext(k)], r3.at[me_d, h], b1_s.at[h], b1_r.at[h], (dnext(k), me))
+
+    def image_sums(h):
+        at = pl.ds(h * kvd, kvd)
+        total = i_own[y, :, at] + i_l1[y, :, at].astype(F32)
+        for k in range(1, ycount):
+            arrived(i_l2.at[k, :, at], rs_s.at[1, k], rs1_r.at[k - 1, h])
+            total = total + i_l2[k, :, at].astype(F32)
+        kvb[h] = (total * sc_i[:, 0:1]).reshape(dp, rb, kvd).astype(BF16)
+        r3[me_d, h] = kvb[h, me_d]
+
+        @pl.loop(1, dp)
+        def _(k):
+            b1(k, h).start()
+
+    arrived(i_l1.at[y], rs_s.at[1, 0], rs_r.at[1, 0])
+    image_sums(0)
     for k in range(1, ycount):
         for which, g in ((0, gk), (1, gv)):
             arrived(g.at[later_rows, col(yprev(k) * 2 + 1 - core)], kbp_s.at[which, k - 1], kbp_r.at[which, k - 1])
     text_far(1)
+    image_sums(1)
     st_t[...] = to_rows(
         jnp.sum(sc_t[...].reshape(tokens, 128), axis=1, keepdims=True),
         jnp.sum(co_t[...].reshape(tokens, 128), axis=1, keepdims=True),
@@ -574,23 +591,29 @@
         vis_chunk(j)
         if j > 0:
             vis_two(j - 1)
-        if j == min(2, pieces - 1):
-
-            arrived(r3.at[others], b1_s.at[0], b1_r.at[0])
+        if j == min(3, pieces - 1):
+
+            for h in range(2):
+                arrived(r3.at[others, h], b1_s.at[h], b1_r.at[h])
 
             extra = jnp.zeros((rb, 2 * kvd), F32)
             for k in range(1, ycount):
                 arrived(tb_y.at[k - 1], tby_s.at[k - 1], tby_r.at[k - 1])
                 extra = extra + tb_y[k - 1].astype(F32)
-            r3[dp] = extra.astype(BF16)
+            r3[dp, 0] = extra[:, :kvd].astype(BF16)
+            r3[dp, 1] = extra[:, kvd:].astype(BF16)
 
             @pl.loop(0, dp)
             def _(d):
                 source = owner_of(d * slots + 1)
                 source = jnp.where(is_filled(d * slots) == 1, owner_of(d * slots), source)
-                s4[d] = r3[jnp.where(d == lone, jnp.int32(dp), source)]
-
-            s5[...] = r3[owner_of(crowded * slots + 1)]
+                source = jnp.where(d == lone, jnp.int32(dp), source)
+                s4[d, :, :kvd] = r3[source, 0]
+                s4[d, :, kvd:] = r3[source, 1]
+
+            source = owner_of(crowded * slots + 1)
+            s5[:, :kvd] = r3[source, 0]
+            s5[:, kvd:] = r3[source, 1]
             r4[0, my_inner, my_outer] = s4[me_d]
             r4[1, my_inner, my_outer] = s5[...]
 
@@ -624,17 +647,19 @@
     lax.fori_loop(0, width // step, text_back, 0)
     vf = vis[...].astype(F32)
     vscale = lax.rsqrt(jnp.mean(vf * vf, axis=1, keepdims=True) + 1e-06)
-    hs = []
+    row_gain = gain_row(vgain)
+    lanes = jnp.zeros((rows, 128), F32)
     for j in range(pieces):
         at = pl.ds(cuts[j], cuts[j + 1] - cuts[j])
         d = d_own[y, :, at] + d_l1[y, :, at].astype(F32)
         for k in range(1, ycount):
             arrived(d_l2.at[k, :, at], dv_s.at[k], dv_r.at[j, k])
             d = d + d_l2[k, :, at].astype(F32)
-        hs.append(d.astype(BF16).astype(F32))
-    h = jnp.concatenate(hs, axis=1) * gain_row(vgain)
-    v_inner = jnp.mean(h * vf, axis=1, keepdims=True)
-    vg_out[...] = (vscale * h - vf * vscale * vscale * vscale * v_inner).astype(BF16)
+        h = d.astype(BF16).astype(F32) * row_gain[:, cuts[j]:cuts[j + 1]]
+        d_own[y, :, at] = h
+        lanes = lanes + fold(h * vis[:, at].astype(F32))
+    v_inner = jnp.sum(lanes, axis=1, keepdims=True) / dv
+    vg_out[...] = (vscale * d_own[y] - vf * (vscale * vscale * vscale * v_inner)).astype(BF16)
 
     arrived(s4.at[others], b2_s.at[0], b2_r.at[0])
     arrived(r4.at[1, 1 - my_inner], b3_s.at[1], b3_r.at[1])
@@ -665,7 +690,8 @@
     for which, (first, second) in enumerate(((kg4, s2k), (vg4, s2v))):
         sent(first.at[:, others], a1_s.at[which])
         sent(second.at[others], a2_s.at[which])
-    sent(kvb.at[others], b1_s.at[0])
+    for h in range(2):
+        sent(kvb.at[h, others], b1_s.at[h])
     sent(s4.at[others], b2_s.at[0])
     sent(r4.at[1, my_inner, pl.ds(0, outer - 1)], b3_s.at[0])
     sent(r4.at[1, my_inner], b3_s.at[1])
@@ -721,12 +747,12 @@
         V((ys - 1, rb, 2 * kvd), BF16), V((ys - 1, rb, 2 * kvd), BF16),
         V((dp * slots, rb, kvd), BF16), V((dp * slots, rb, kvd), BF16),
         V((dp, rb, kvd), BF16), V((dp, rb, kvd), BF16), V((dp, rb, kvd), BF16), V((dp, rb, kvd), BF16),
-        V((dp, rb, 2 * kvd), BF16), V((dp + 1, rb, 2 * kvd), BF16),
+        V((2, dp, rb, kvd), BF16), V((dp + 1, 2, rb, kvd), BF16),
         V((dp, rb, 2 * kvd), BF16), V((rb, 2 * kvd), BF16), V((2, 2, dp // 2, rb, 2 * kvd), BF16),
-        DMA((9,)), DMA((5, 2 * ys - 1)), DMA((5, 2 * ys - 1)), DMA((2, ys)), DMA((2, ys)), DMA((ys - 1,)),
+        DMA((9,)), DMA((5, 2 * ys - 1)), DMA((5, 2 * ys - 1)), DMA((2, ys)), DMA((2, ys)), DMA((ys - 1, 2)),
         DMA((ys - 1, 2)), DMA((3,)), DMA((3,)), DMA((ys,)), DMA((pieces, ys)),
         DMA((2,)), DMA((2,)), DMA((2,)), DMA((2,)),
-        DMA((1,)), DMA((1,)), DMA((1,)), DMA((1,)), DMA((2,)), DMA((2,)),
+        DMA((2,)), DMA((2,)), DMA((1,)), DMA((1,)), DMA((2,)), DMA((2,)),
         DMA((ys - 1,)), DMA((ys - 1,)), DMA((1,)), DMA((1,)), DMA((2, ys - 1)), DMA((2, ys - 1)),
         DMA((1,)), DMA((1,)), DMA((ys - 1,)), DMA((ys - 1,)), V((slots, PATCH, width), F32),
     ]

time: 61.1 us -> 59.2 us (0.969)
  Pallas kernels: 60.1 us -> 58.2 us
    pallas_call x1, Pallas kernels: 58.4 us -> 56.6 us  [shards(): pl.pallas_call(functools.partial(kernel, dp, mp), out_shape=tuple((V(shap...]
where the time goes in v5:
time: 59.2 us; the launch traced here: 59 us
  Pallas kernels  58.2 us (98%)
  between operations  0.8 us (1%)
    pallas_call x1, Pallas kernels, shards(): pl.pallas_call(functools.partial(kernel, dp, mp), out_shape=tuple((V(shap...  56.6 us
    pallas_call x1, Pallas kernels, shards(): pl.pallas_call(write_out, out_shape=tuple((jax.ShapeDtypeStruct(shape, BF...  1.65 us

profile of v5, /device:TPU:0, one launch (start us, length us, event | category | flops | bytes accessed | tf_op | source)
XLA Modules:
  0.0 59.0 jit_solution(6478100064924650062)
XLA Ops:
  0.6 56.6 %shard_map.129 = (bf16[512,256]{1,0:T(8,128)(2,1)S(1)}, bf16[512,256]{1,0:T(8,128)(2,1)S(1)}, bf16[512,2048]{1,0:T(8,128)(2,1)S(1)}, bf16[64,3200]{1,0:T(8,128)(2,1)S(1)}) custom-call(s32[8]{0:T(128)} %slot_ref.1, bf16[64,3200]{1,0:T(8,128)(2,1)} %vision_h.1, f32[25,128]{1,0:T(8,128)} %bitcast.12, bf16[2,256,2048]{2,1,0:T(8,128)(2,1)} %bitcast.7, ...), custom_call_target="tpu_custom_call" | custom-call | tf_op jit(solution)/shard_map/pallas_call | solution.py:762
  57.2 1.7 %shard_map.130 = (bf16[512,256]{1,0:T(8,128)(2,1)}, bf16[512,256]{1,0:T(8,128)(2,1)}, bf16[512,2048]{1,0:T(8,128)(2,1)}, bf16[64,3200]{1,0:T(8,128)(2,1)}) custom-call(bf16[512,256]{1,0:T(8,128)(2,1)S(1)} %get-tuple-element.8.refs_0_, bf16[512,256]{1,0:T(8,128)(2,1)S(1)} %get-tuple-element.9.refs_1_, bf16[512,2048]{1,0:T(8,128)(2,1)S(1)} %get-tuple-element.10.refs_2_, ...), custom_call_target="tpu_custom_call" | custom-call | tf_op jit(solution)/shard_map/pallas_call | solution.py:776

commit v6 on v5

--- a/solution.py
+++ b/solution.py
@@ -581,17 +581,17 @@
 
     def b3(k):
         target = lax.rem(my_outer + k, outer) * inner + my_inner
-        return remote(s5, r4.at[1, my_inner, my_outer], b3_s.at[0], b3_r.at[0], (target, me))
-
-    def b4():
-        block = r4.at[1, my_inner]
-        return remote(block, block, b3_s.at[1], b3_r.at[1], (my_outer * inner + 1 - my_inner, me))
+        return remote(s5, r4.at[1, my_inner, my_outer], b3_s.at[0], b3_r.at[k], (target, me))
+
+    def b4(k):
+        block = r4.at[1, my_inner, lax.rem(my_outer + outer - k, outer)]
+        return remote(block, block, b3_s.at[1], b3_r.at[0], (my_outer * inner + 1 - my_inner, me))
 
     for j in range(pieces):
         vis_chunk(j)
         if j > 0:
             vis_two(j - 1)
-        if j == min(3, pieces - 1):
+        if j == min(4, pieces - 1):
 
             for h in range(2):
                 arrived(r3.at[others, h], b1_s.at[h], b1_r.at[h])
@@ -617,17 +617,19 @@
             r4[0, my_inner, my_outer] = s4[me_d]
             r4[1, my_inner, my_outer] = s5[...]
 
-            @pl.loop(1, outer)
-            def _(k):
+            for k in range(1, outer):
                 b3(k).start()
 
             @pl.loop(1, dp)
             def _(k):
                 b2(k).start()
 
+            start(s5, r4.at[1, my_inner, my_outer], b3_s.at[1], b3_r.at[0], (my_outer * inner + 1 - my_inner, me))
+
     vis_two(pieces - 1)
-    arrived(r4.at[1, my_inner, pl.ds(0, outer - 1)], b3_s.at[0], b3_r.at[0])
-    b4().start()
+    for k in range(1, outer):
+        arrived(r4.at[1, my_inner, lax.rem(my_outer + outer - k, outer)], b3_s.at[0], b3_r.at[k])
+        b4(k).start()
     sq_t, inner_t = stats_total(0, st_t, sr_t)
     keep = jnp.concatenate([jnp.full((PATCH, 1), 1.0, F32) * keeps[p] for p in range(slots)], axis=0)
     scale_t = lax.rsqrt(sq_t / d_model + 1e-05)
@@ -645,6 +647,17 @@
         return 0
 
     lax.fori_loop(0, width // step, text_back, 0)
+    arrived(t_l1.at[y], rs_s.at[0, 0], rs_r.at[0, 0])
+    for p in range(t_pieces):
+        for k in range(1, ycount):
+            text_piece(p, k).wait_recv()
+    direct = t_l2[1].astype(F32)
+    for k in range(2, ycount):
+        direct = direct + t_l2[k].astype(F32)
+    for s in range(slots):
+        at = place_of[s]
+        total = t_own[y, at] + t_l1[y, at].astype(F32) + direct * (1.0 - at.astype(F32))
+        dt[s, :, :2 * kvd] = total * sc_t[at][:, 0:1]
     vf = vis[...].astype(F32)
     vscale = lax.rsqrt(jnp.mean(vf * vf, axis=1, keepdims=True) + 1e-06)
     row_gain = gain_row(vgain)
@@ -662,22 +675,13 @@
     vg_out[...] = (vscale * d_own[y] - vf * (vscale * vscale * vscale * v_inner)).astype(BF16)
 
     arrived(s4.at[others], b2_s.at[0], b2_r.at[0])
-    arrived(r4.at[1, 1 - my_inner], b3_s.at[1], b3_r.at[1])
-
-    arrived(t_l1.at[y], rs_s.at[0, 0], rs_r.at[0, 0])
-    for p in range(t_pieces):
-        for k in range(1, ycount):
-            text_piece(p, k).wait_recv()
-    direct = t_l2[1].astype(F32)
-    for k in range(2, ycount):
-        direct = direct + t_l2[k].astype(F32)
+    arrived(r4.at[1, 1 - my_inner], b3_s.at[1], b3_r.at[0])
+
     for s in range(slots):
-        at = place_of[s]
-        is_first = 1.0 - at.astype(F32)
         which = s * first_holds * second_holds
         placed = jnp.concatenate([r4[which, r % inner, r // inner] for r in range(dp)], axis=0).astype(F32)
-        total = t_own[y, at] + t_l1[y, at].astype(F32) + direct * is_first + placed * ((1.0 - is_first) * at_lone)
-        out = total * sc_t[at][:, 0:1] + placed * filled[s]
+        share = sc_t[place_of[s]][:, 0:1] * (place_of[s].astype(F32) * at_lone) + filled[s]
+        out = dt[s, :, :2 * kvd] + placed * share
         rows_s = pl.ds(s * PATCH, PATCH)
         k_out[rows_s, :] = out[:, :kvd].astype(BF16)
         v_out[rows_s, :] = out[:, kvd:].astype(BF16)
@@ -752,7 +756,7 @@
         DMA((9,)), DMA((5, 2 * ys - 1)), DMA((5, 2 * ys - 1)), DMA((2, ys)), DMA((2, ys)), DMA((ys - 1, 2)),
         DMA((ys - 1, 2)), DMA((3,)), DMA((3,)), DMA((ys,)), DMA((pieces, ys)),
         DMA((2,)), DMA((2,)), DMA((2,)), DMA((2,)),
-        DMA((2,)), DMA((2,)), DMA((1,)), DMA((1,)), DMA((2,)), DMA((2,)),
+        DMA((2,)), DMA((2,)), DMA((1,)), DMA((1,)), DMA((2,)), DMA((dp // 2,)),
         DMA((ys - 1,)), DMA((ys - 1,)), DMA((1,)), DMA((1,)), DMA((2, ys - 1)), DMA((2, ys - 1)),
         DMA((1,)), DMA((1,)), DMA((ys - 1,)), DMA((ys - 1,)), V((slots, PATCH, width), F32),
     ]

time: 59.2 us -> 58.7 us (level)
  no operation moved by 1% of the time
where the time goes in v6:
time: 58.7 us; the launch traced here: 58.5 us
  Pallas kernels  57.7 us (98%)
  between operations  0.8 us (1%)
    pallas_call x1, Pallas kernels, shards(): pl.pallas_call(functools.partial(kernel, dp, mp), out_shape=tuple((V(shap...  56 us
    pallas_call x1, Pallas kernels, shards(): pl.pallas_call(write_out, out_shape=tuple((jax.ShapeDtypeStruct(shape, BF...  1.65 us

profile of v6, /device:TPU:0, one launch (start us, length us, event | category | flops | bytes accessed | tf_op | source)
XLA Modules:
  0.0 58.5 jit_solution(5910083066407297654)
XLA Ops:
  0.6 56.0 %shard_map.129 = (bf16[512,256]{1,0:T(8,128)(2,1)S(1)}, bf16[512,256]{1,0:T(8,128)(2,1)S(1)}, bf16[512,2048]{1,0:T(8,128)(2,1)S(1)}, bf16[64,3200]{1,0:T(8,128)(2,1)S(1)}) custom-call(s32[8]{0:T(128)} %slot_ref.1, bf16[64,3200]{1,0:T(8,128)(2,1)} %vision_h.1, f32[25,128]{1,0:T(8,128)} %bitcast.12, bf16[2,256,2048]{2,1,0:T(8,128)(2,1)} %bitcast.7, ...), custom_call_target="tpu_custom_call" | custom-call | tf_op jit(solution)/shard_map/pallas_call | solution.py:766
  56.7 1.7 %shard_map.130 = (bf16[512,256]{1,0:T(8,128)(2,1)}, bf16[512,256]{1,0:T(8,128)(2,1)}, bf16[512,2048]{1,0:T(8,128)(2,1)}, bf16[64,3200]{1,0:T(8,128)(2,1)}) custom-call(bf16[512,256]{1,0:T(8,128)(2,1)S(1)} %get-tuple-element.8.refs_0_, bf16[512,256]{1,0:T(8,128)(2,1)S(1)} %get-tuple-element.9.refs_1_, bf16[512,2048]{1,0:T(8,128)(2,1)S(1)} %get-tuple-element.10.refs_2_, ...), custom_call_target="tpu_custom_call" | custom-call | tf_op jit(solution)/shard_map/pallas_call | solution.py:780

commit v7 on v6

--- a/solution.py
+++ b/solution.py
@@ -72,7 +72,7 @@
     d_send, d_own, d_l1, d_s2, d_l2,
     st_t, sr_t, st_i, sr_i, st_q, sr_q, sc_t, co_t, sc_i, co_i,
     kgs, vgs, kb_send, kb_y, kbr, tb_send, tb_recv, tb_sel, tb_y,
-    r1k, r1v, s2k, s2v, r2k, r2v, kvb, r3, s4, s5, r4,
+    r1k, r1v, s2k, s2v, r2k, r2v, kvb, r3, s4, s5, r4, sources,
     load_sem, ag_s, ag_r, rs_s, rs_r, rs1_r, t2_r, st_s, st_r, dv_s, dv_r,
     a1_s, a1_r, a2_s, a2_r, b1_s, b1_r, b2_s, b2_r, b3_s, b3_r, kby_s, kby_r, kbz_s, kbz_r, kbp_s, kbp_r,
     tbz_s, tbz_r, tby_s, tby_r, dt,
@@ -360,7 +360,6 @@
     lax.fori_loop(0, width // step // 2, text_near, 0)
     lax.fori_loop(width // step // 2, width // step, text_near, 0)
     co_t[...] = jnp.zeros(co_t.shape, F32)
-    gather_relay(0, vis_block)
     def survey(d, found):
         count = jnp.int32(0)
         for i in range(dp):
@@ -370,6 +369,14 @@
     lone, crowded = lax.fori_loop(0, dp, survey, (jnp.int32(0), jnp.int32(0)))
     lone_slot = lone * slots + 1
     at_lone = keeps[1]
+
+    @pl.loop(0, dp)
+    def _(d):
+        source = owner_of(d * slots + 1)
+        source = jnp.where(is_filled(d * slots) == 1, owner_of(d * slots), source)
+        sources[d] = jnp.where(d == lone, jnp.int32(dp), source)
+
+    gather_relay(0, vis_block)
     loads[7].wait()
     loads[8].wait()
 
@@ -605,9 +612,7 @@
 
             @pl.loop(0, dp)
             def _(d):
-                source = owner_of(d * slots + 1)
-                source = jnp.where(is_filled(d * slots) == 1, owner_of(d * slots), source)
-                source = jnp.where(d == lone, jnp.int32(dp), source)
+                source = sources[d]
                 s4[d, :, :kvd] = r3[source, 0]
                 s4[d, :, kvd:] = r3[source, 1]
 
@@ -752,7 +757,7 @@
         V((dp * slots, rb, kvd), BF16), V((dp * slots, rb, kvd), BF16),
         V((dp, rb, kvd), BF16), V((dp, rb, kvd), BF16), V((dp, rb, kvd), BF16), V((dp, rb, kvd), BF16),
         V((2, dp, rb, kvd), BF16), V((dp + 1, 2, rb, kvd), BF16),
-        V((dp, rb, 2 * kvd), BF16), V((rb, 2 * kvd), BF16), V((2, 2, dp // 2, rb, 2 * kvd), BF16),
+        V((dp, rb, 2 * kvd), BF16), V((rb, 2 * kvd), BF16), V((2, 2, dp // 2, rb, 2 * kvd), BF16), pltpu.SMEM((dp,), jnp.int32),
         DMA((9,)), DMA((5, 2 * ys - 1)), DMA((5, 2 * ys - 1)), DMA((2, ys)), DMA((2, ys)), DMA((ys - 1, 2)),
         DMA((ys - 1, 2)), DMA((3,)), DMA((3,)), DMA((ys,)), DMA((pieces, ys)),
         DMA((2,)), DMA((2,)), DMA((2,)), DMA((2,)),

time: 58.7 us -> 58.7 us (level)
  no operation moved by 1% of the time
where the time goes in v7:
time: 58.7 us; the launch traced here: 58.5 us
  Pallas kernels  57.7 us (98%)
  between operations  0.8 us (1%)
    pallas_call x1, Pallas kernels, shards(): pl.pallas_call(functools.partial(kernel, dp, mp), out_shape=tuple((V(shap...  56.1 us
    pallas_call x1, Pallas kernels, shards(): pl.pallas_call(write_out, out_shape=tuple((jax.ShapeDtypeStruct(shape, BF...  1.65 us

profile of v7, /device:TPU:0, one launch (start us, length us, event | category | flops | bytes accessed | tf_op | source)
XLA Modules:
  0.0 58.5 jit_solution(16246022306447385941)
XLA Ops:
  0.6 56.1 %shard_map.129 = (bf16[512,256]{1,0:T(8,128)(2,1)S(1)}, bf16[512,256]{1,0:T(8,128)(2,1)S(1)}, bf16[512,2048]{1,0:T(8,128)(2,1)S(1)}, bf16[64,3200]{1,0:T(8,128)(2,1)S(1)}) custom-call(s32[8]{0:T(128)} %slot_ref.1, bf16[64,3200]{1,0:T(8,128)(2,1)} %vision_h.1, f32[25,128]{1,0:T(8,128)} %bitcast.12, bf16[2,256,2048]{2,1,0:T(8,128)(2,1)} %bitcast.7, ...), custom_call_target="tpu_custom_call" | custom-call | tf_op jit(solution)/shard_map/pallas_call | solution.py:771
  56.7 1.7 %shard_map.130 = (bf16[512,256]{1,0:T(8,128)(2,1)}, bf16[512,256]{1,0:T(8,128)(2,1)}, bf16[512,2048]{1,0:T(8,128)(2,1)}, bf16[64,3200]{1,0:T(8,128)(2,1)}) custom-call(bf16[512,256]{1,0:T(8,128)(2,1)S(1)} %get-tuple-element.8.refs_0_, bf16[512,256]{1,0:T(8,128)(2,1)S(1)} %get-tuple-element.9.refs_1_, bf16[512,2048]{1,0:T(8,128)(2,1)S(1)} %get-tuple-element.10.refs_2_, ...), custom_call_target="tpu_custom_call" | custom-call | tf_op jit(solution)/shard_map/pallas_call | solution.py:785
